TPU v7x, 128 devices: a whole 4x4x4 slice. The times are simulated.
128 devices in a mesh: group: 8 (over z, core), pair: 16 (over y, x).
Axes of the slice: x: 4, y: 4, z: 4, core: 2. Of those that a mesh axis runs over, the one named last changes fastest.
Arguments:
- query_embed: bfloat16 [8, 16, 1024], P('group'), may hold values from -6 to 6
- teacher_scores: float32 [8, 16, 16, 32], P('group', 'pair'), may hold values from -9 to 9
- pair_owner: int32 [8, 16, 16, 32, 1], P('group', 'pair'), may hold values from 0 to 127; in each aligned block of 512 rows (0 to 511, 512 to 1023, ..., all dimensions but the last counted through in order) at most 8 rows name the same one
- pair_row: int32 [8, 16, 16, 32], P('group', 'pair'), may hold values from 0 to 2047
- passage_hidden: bfloat16 [262144, 1024], P(('group', 'pair')), may hold values from -24 to 24
- projection: bfloat16 [1024, 1024], replicated, may hold values from -0.1875 to 0.1875
Outputs:
- query_loss: float32 [8, 16], P('group', 'pair')
- query_grad: float32 [8, 16, 1024], P('group', 'pair')
- hidden_grad: bfloat16 [262144, 1024], P(('group', 'pair'))
- projection_grad: float32 [1024, 1024], P(('group', 'pair'))
Inputs may be any that keep to these rules, and one draw needn't show every extreme that they name: `pair_owner`: owners are numbered with group as the slower index. Among the 512 candidates held by one device, at most 8 name the same owner, and every draw has a device and an owner with exactly 8. `pair_row`: A passage may be named by several candidates.
All inputs are finite; a program needn't handle non-finite values.
Results may differ from a plain program's by a relative error of at most 0.022.
Values may be sent and summed in bfloat16 or wider, within the bound.
A program may use at most 128 MiB of HBM per device.

v0:
```python
import math

import jax
import jax.numpy as jnp
from jax import lax
from jax.sharding import PartitionSpec as P

loss_scale = 1024.0


def soft_steps(values_all, values_own):
    return jax.nn.sigmoid((values_all[:, None, :] - values_own[:, :, None]) * 2.0)


def score_slope(soft_step, grad_all, grad_own):
    slopes = soft_step * (1.0 - soft_step)
    return 2.0 * (jnp.sum(slopes * grad_all[:, None, :], -1) - grad_own * jnp.sum(slopes, -1))


def shards(query_embed, teacher_scores, pair_owner, pair_row, passage_hidden, projection):
    model_width = query_embed.shape[2]
    query_rows = query_embed.shape[1]
    cand_dev = teacher_scores.shape[3]
    pass_rows = passage_hidden.shape[0]
    pair_size = lax.axis_size("pair")
    group_size = lax.axis_size("group")
    devices = pair_size * group_size
    cand_all = cand_dev * pair_size
    pair_count = query_rows * cand_dev
    capacity = max(2, 2 * pair_count // devices)
    query_dev = query_rows // pair_size
    inv_root = 1.0 / math.sqrt(model_width)
    spearman_den = float(cand_all * (cand_all * cand_all - 1))
    embedded = jnp.dot(passage_hidden, projection, preferred_element_type=jnp.float32).astype(
        jnp.bfloat16
    )
    owner_dev = pair_owner.reshape(pair_count)
    row_index = pair_row.reshape(pair_count)
    owner_marks = (owner_dev[:, None] == jnp.arange(devices, dtype=jnp.int32)[None, :]).astype(
        jnp.int32
    )
    slot_index = jnp.sum(jnp.cumsum(owner_marks, axis=0) * owner_marks, axis=1) - 1
    requests = jnp.zeros((devices, capacity), jnp.int32).at[owner_dev, slot_index].set(row_index)
    queries = query_embed[0]
    asked_rows = lax.all_to_all(
        requests, ("group", "pair"), split_axis=0, concat_axis=0, tiled=True
    )
    vectors = jnp.take(embedded, asked_rows, axis=0)
    replies = lax.all_to_all(vectors, ("group", "pair"), split_axis=0, concat_axis=0, tiled=True)
    pair_vectors = replies[owner_dev, slot_index].reshape(query_rows, cand_dev, model_width)
    scores = (
        jnp.einsum("qd,qcd->qc", queries, pair_vectors, preferred_element_type=jnp.float32)
        * inv_root
    )
    teacher_own = teacher_scores.reshape(query_rows, cand_dev)
    scores_all, teacher_all = (
        lax.all_gather(scores, "pair", axis=1, tiled=True),
        lax.all_gather(teacher_own, "pair", axis=1, tiled=True),
    )
    soft_step = soft_steps(scores_all, scores)
    rank_student = 0.5 + jnp.sum(soft_step, -1)
    rank_teacher = 0.5 + jnp.sum(soft_steps(teacher_all, teacher_own), -1)
    rank_gap = rank_student - rank_teacher
    loss_part = 6.0 * jnp.sum(rank_gap * rank_gap, axis=1) / spearman_den
    rank_grad = loss_scale * 12.0 * rank_gap / spearman_den
    grad_all = lax.all_gather(rank_grad, "pair", axis=1, tiled=True)
    score_grad = score_slope(soft_step, grad_all, rank_grad)
    query_part = (
        jnp.sum(score_grad[:, :, None] * pair_vectors.astype(jnp.float32), axis=1) * inv_root
    )
    pair_grad = (
        score_grad[:, :, None] * queries.astype(jnp.float32)[:, None, :] * inv_root
    ).astype(jnp.bfloat16)
    query_sum, loss_own = (
        lax.psum_scatter(
            query_part.astype(jnp.bfloat16), "pair", scatter_dimension=0, tiled=True
        ).astype(jnp.float32),
        lax.psum_scatter(
            loss_part.astype(jnp.bfloat16), "pair", scatter_dimension=0, tiled=True
        ).astype(jnp.float32),
    )
    outgoing = (
        jnp.zeros((devices, capacity, model_width), jnp.bfloat16)
        .at[owner_dev, slot_index]
        .set(pair_grad.reshape(pair_count, model_width))
    )
    arrived = lax.all_to_all(outgoing, ("group", "pair"), split_axis=0, concat_axis=0, tiled=True)
    embed_grad = (
        jnp.zeros((pass_rows, model_width), jnp.float32)
        .at[asked_rows.reshape(-1)]
        .add(arrived.reshape(-1, model_width).astype(jnp.float32))
    )
    grad_rounded = embed_grad.astype(jnp.bfloat16)
    hidden_grad = jnp.einsum(
        "pe,de->pd", grad_rounded, projection, preferred_element_type=jnp.float32
    ).astype(jnp.bfloat16)
    projection_grad = lax.psum_scatter(
        jnp.einsum("pr,pe->re", passage_hidden, grad_rounded, preferred_element_type=jnp.float32),
        ("group", "pair"),
        scatter_dimension=0,
        tiled=True,
    )
    return (
        loss_own.reshape(1, query_dev),
        query_sum.reshape(1, query_dev, model_width),
        hidden_grad,
        projection_grad,
    )


def solution(mesh):
    placed = (
        P("group", None, None),
        P("group", "pair", None, None),
        P("group", "pair", None, None, None),
        P("group", "pair", None, None),
        P(("group", "pair"), None),
        P(),
    )
    return jax.shard_map(
        shards,
        mesh=mesh,
        in_specs=placed,
        out_specs=(
            P("group", "pair"),
            P("group", "pair", None),
            P(("group", "pair"), None),
            P(("group", "pair"), None),
        ),
        check_vma=False,
    )
```

profile of v0, /device:TPU:0, one launch (start us, length us, event | category | flops | bytes accessed | tf_op | source)
XLA Modules:
  0.0 964.1 jit_solution(8039499689911197415)
XLA Ops:
  7.2 0.9 eq.25
  8.1 0.8 eq.29
  8.9 0.8 reshape.243
  9.7 0.5 broadcast.268
  10.2 1.4 reduce.10
  11.5 0.1 reshape.209
  11.6 0.1 copy.29
  11.7 0.2 fusion.12
  12.0 0.2 fusion.11
  12.3 22.0 %scatter_fusion = s32[128,8]{0,1:T(8,128)S(1)} fusion(s32[128,8]{0,1:T(8,128)S(1)} %broadcast_in_dim.18, s32[512]{0:T(512)S(1)} %bitcast.82, s32[512]{0:T(512)S(1)} %reshape.243), kind=kCustom, calls=%fused_computation.2 | custom fusion | bytes 10240 | tf_op jit(solution)/shard_map/scatter | solution.py:43
  34.3 0.7 copy.31
  35.0 11.1 %all-to-all-start = ((s32[128,1,8]{2,1,0:T(1,128)}), s32[128,1,8]{2,1,0:T(1,128)S(1)}, u32[]{:S(2)}, u32[]{:S(2)}) async-start(s32[128,1,8]{2,1,0:T(1,128)} %copy.31), calls=%async_computation | async-start | bytes 131072 | tf_op jit(solution)/shard_map/all_to_all | solution.py:45
  46.2 8.3 convolution_convert_fusion.1
  54.5 1.2 all-to-all-done
  55.7 0.1 copy.33
  55.9 0.1 reshape.229
  56.0 8.8 gather_fusion
  64.7 3.2 bitcast_select_fusion
  67.9 9.1 all-to-all-start.1
  77.1 41.4 %all-gather = f32[1,1,16,512]{2,1,0,3:T(1,128)S(1)} all-gather(f32[1,1,16,32]{2,1,0,3:T(1,128)S(1)} %copy.35), channel_id=2, replica_groups=mesh['group'=8,'pair'=16] {'pair'}, dimensions={3}, use_global_device_ids=true | all-gather | bytes 34816 | tf_op jit(solution)/shard_map/all_gather | solution.py:58
  118.5 0.1 copy.36
  118.6 0.4 fusion.8
  119.1 7.7 gather_fusion.1
  126.8 0.4 fusion.15
  127.2 21.9 %all-gather.1 = f32[16,32,16]{1,2,0:T(8,128)S(1)} all-gather(f32[1,32,16]{1,2,0:T(8,128)S(1)} %get-tuple-element.28), channel_id=1, replica_groups=mesh['group'=8,'pair'=16] {'pair'}, dimensions={0}, use_global_device_ids=true | all-gather | bytes 34816 | tf_op jit(solution)/shard_map/all_gather | solution.py:57
  149.2 0.1 reshape.264
  149.3 0.6 fusion.9
  149.9 22.6 %all-gather.2 = f32[16,32,16]{1,2,0:T(8,128)S(1)} all-gather(f32[1,32,16]{1,2,0:T(8,128)S(1)} %multiply_bitcast_fusion), channel_id=1, replica_groups=mesh['group'=8,'pair'=16] {'pair'}, dimensions={0}, use_global_device_ids=true | all-gather | bytes 34816 | tf_op jit(solution)/shard_map/all_gather | solution.py:66
  172.6 0.1 reshape.266
  172.7 0.5 multiply_reduce_fusion.1
  173.2 0.1 subtract_multiply_fusion.1
  173.4 1.2 fusion.5
  174.6 1.6 broadcast_in_dim.23
  176.2 73.0 %scatter_fusion.1 = bf16[128,8,1024]{2,1,0:T(8,128)(2,1)} fusion(bf16[128,8,1024]{2,1,0:T(8,128)(2,1)} %broadcast_in_dim.23, s32[512]{0:T(512)S(1)} %bitcast.83, bf16[512,1024]{1,0:T(8,128)(2,1)} %fusion.5), kind=kCustom, calls=%fused_computation.3 | custom fusion | bytes 3149824 | tf_op jit(solution)/shard_map/scatter | solution.py:85
  249.2 8.3 all-to-all-start.2
  257.6 0.8 reduce.11
  258.4 0.1 reshape.218
  258.5 28.3 %all-to-all-done.2 = bf16[128,8,1024]{2,1,0:T(8,128)(2,1)} async-done(((bf16[128,8,1024]{2,1,0:T(8,128)(2,1)}), bf16[128,8,1024]{2,1,0:T(8,128)(2,1)}, u32[]{:S(2)}, u32[]{:S(2)}) %all-to-all-start.2) | async-done | bytes 2097184 | tf_op jit(solution)/shard_map/all_to_all | solution.py:87
  286.8 13.4 %scatter_custom_fusion.2 = f32[2048,1024]{1,0:T(8,128)} fusion(s32[1024]{0:T(1024)S(1)} %bitcast.101, f32[]{:T(128)} %constant.26.clone.1, bf16[128,8,1024]{2,1,0:T(8,128)(2,1)} %all-to-all-done.2), kind=kCustom, calls=%fused_computation.5 | custom fusion | flops 2097152 | bytes 10485764 | tf_op jit(solution)/shard_map/scatter-add | solution.py:91
  300.2 11.2 %convolution_bitcast_fusion = f32[1024,1024]{0,1:T(8,128)} fusion(bf16[2048,1024]{1,0:T(8,128)(2,1)} %param.10, f32[2048,1024]{1,0:T(8,128)} %scatter_custom_fusion.2), kind=kOutput, calls=%fused_computation.10 | convolution fusion | flops 4297064448 | bytes 16777216 | tf_op jit(solution)/shard_map/pr,pe->re/dot_general | solution.py:98
  311.4 5.3 copy.41
  316.7 0.5 multiply_reduce_fusion
  317.3 0.6 dynamic-slice
  317.9 72.1 %all-reduce.2 = (bf16[16]{0:T(256)(128)(2,1)S(1)}, bf16[16,1024]{1,0:T(8,128)(2,1)S(1)}) all-reduce(bf16[16]{0:T(256)(128)(2,1)S(1)} %multiply_convert_fusion.1, bf16[16,1024]{1,0:T(8,128)(2,1)S(1)} %multiply_convert_fusion), channel_id=3, replica_groups=mesh['group'=8,'pair'=16] {'pair'}, use_global_device_ids=true, to_apply=%region_7.8.clone | all-reduce | flops 16400 | bytes 65600
  390.1 1.2 dynamic-slice.1
  391.9 1.2 bitcast_convert_fusion.1
  393.2 9.5 convolution_convert_fusion
  402.7 553.5 %reduce-scatter.4.cloned.1.call-done = f32[8,1024]{1,0:T(8,128)} async-done(((f32[1024,1024]{1,0:T(8,128)}), f32[8,1024]{1,0:T(8,128)}) %reduce-scatter.4.cloned.1.call-update) | async-done | bytes 32784
  (34 shorter events, 0.6 us)
Async XLA Ops:
  7.2 39.0 %copy-start = (bf16[1024,1024]{1,0:T(8,128)(2,1)S(1)}, bf16[1024,1024]{1,0:T(8,128)(2,1)}, u32[]{:S(2)}) copy-start(bf16[1024,1024]{1,0:T(8,128)(2,1)} %param.11) | copy-start | bytes 6291460
  35.0 20.6 %all-to-all-start = ((s32[128,1,8]{2,1,0:T(1,128)}), s32[128,1,8]{2,1,0:T(1,128)S(1)}, u32[]{:S(2)}, u32[]{:S(2)}) async-start(s32[128,1,8]{2,1,0:T(1,128)} %copy.31), calls=%async_computation | async-start | bytes 131072 | tf_op jit(solution)/shard_map/all_to_all | solution.py:45
  64.7 12.3 %copy-start.2 = (f32[1,1,16,32]{3,2,1,0:T(8,128)S(1)}, f32[1,1,16,32]{3,2,1,0:T(8,128)}, u32[]{:S(2)}) copy-start(f32[1,1,16,32]{3,2,1,0:T(8,128)} %param.7) | copy-start | bytes 6148
  64.7 53.9 %copy-start.1 = (bf16[1,16,1024]{2,1,0:T(8,128)(2,1)S(1)}, bf16[1,16,1024]{2,1,0:T(8,128)(2,1)}, u32[]{:S(2)}) copy-start(bf16[1,16,1024]{2,1,0:T(8,128)(2,1)} %param.6) | copy-start | bytes 98308
  67.9 51.1 %all-to-all-start.1 = ((bf16[128,8,1024]{2,1,0:T(8,128)(2,1)}), bf16[128,8,1024]{2,1,0:T(8,128)(2,1)}, u32[]{:S(2)}, u32[]{:S(2)}) async-start(bf16[128,8,1024]{2,1,0:T(8,128)(2,1)} %bitcast_select_fusion), calls=%async_computation.1 | async-start | bytes 4194304 | tf_op jit(solution)/shard_map/all_to_all | solution.py:49
  249.2 37.6 %all-to-all-start.2 = ((bf16[128,8,1024]{2,1,0:T(8,128)(2,1)}), bf16[128,8,1024]{2,1,0:T(8,128)(2,1)}, u32[]{:S(2)}, u32[]{:S(2)}) async-start(bf16[128,8,1024]{2,1,0:T(8,128)(2,1)} %scatter_fusion.1), calls=%async_computation.2 | async-start | bytes 4194304 | tf_op jit(solution)/shard_map/all_to_all | solution.py:87
  257.5 698.6 %reduce-scatter.4.cloned.1.call-start = ((), (), s32[]{:S(2)}) async-start(), calls=%async_computation.4 | async-start | bytes 4227072
  316.7 0.7 copy-start.3
Sparse Core Ops, SparseCore 0:
  316.8 639.2 reduce-scatter.3
where the time goes:
time: 968 us; the launch traced here: 964 us
  waiting for transfers between devices  583 us (60%)
  blocking collectives  158 us (16%)
  local copies, waits for them, and re-layouts  125 us (13%)
  matrix products  29.3 us (3%)
  starting transfers between devices  28.6 us (3%)
  other arithmetic  24 us (2%)
  between operations  16.1 us (2%)
    unnamed x2, waiting for transfers between devices  553 us
    scatter x1, local copies, waits for them, and re-layouts, shards(): outgoing = jnp.zeros((devices, capacity, model_width), jnp.bfloat16).at[o...  73 us
    unnamed x1, blocking collectives  72.1 us
    all_gather x1, blocking collectives, shards(): lax.all_gather(teacher_own, 'pair', axis=1, tiled=True)  41.4 us
    all_to_all x1, waiting for transfers between devices, shards(): lax.all_to_all(outgoing, ('group', 'pair'), split_axis=0, concat_axis=0,...  28.3 us
    all_gather x1, blocking collectives, shards(): grad_all = lax.all_gather(rank_grad, 'pair', axis=1, tiled=True)  22.6 us
    scatter x1, local copies, waits for them, and re-layouts, shards(): jnp.zeros((devices, capacity), jnp.int32).at[owner_dev, slot_index]  22 us
    all_gather x1, blocking collectives, shards(): lax.all_gather(scores, 'pair', axis=1, tiled=True)  21.9 us
  transfers between devices with their start and end apart: 4, of which 3 were waited for; matrix products, arithmetic and copies ran while one was open for 2% of the time, Pallas kernels for 0%

commit v1 on v0

v1 whole, which is shorter than its diff:
```python
import math

import jax
import jax.numpy as jnp
from jax import lax
from jax.sharding import PartitionSpec as P

loss_scale = 1024.0
f32, bf16, i32 = jnp.float32, jnp.bfloat16, jnp.int32


def iota(shape, dim):
    return lax.broadcasted_iota(i32, shape, dim)


def dot(a, b, ca, cb):
    return lax.dot_general(a, b, (((ca,), (cb,)), ((), ())), preferred_element_type=f32)


def halves(x):
    high = x.astype(bf16)
    return high, (x - high.astype(f32)).astype(bf16)


def shards(query_embed, teacher_scores, pair_owner, pair_row, passage_hidden, projection):
    width = query_embed.shape[2]
    q_rows = query_embed.shape[1]
    cand = teacher_scores.shape[3]
    n_pair, n_group = lax.axis_size("pair"), lax.axis_size("group")
    n_dev = n_pair * n_group
    cap = max(2, 2 * q_rows * cand // n_dev)
    slots = n_pair * cap
    k_all = cand * n_pair
    queries_n = n_group * q_rows
    rows = passage_hidden.shape[0]
    den = float(k_all * (k_all * k_all - 1))
    inv_root = 1.0 / math.sqrt(width)
    r = lax.axis_index("pair")
    owner = pair_owner.reshape(1, q_rows * cand)
    row = pair_row.reshape(1, q_rows * cand)
    n_own = q_rows * cand
    lane = iota((1, n_own), 1)
    owner_hot = iota((n_dev, n_own), 0) == owner
    owner_b = owner_hot.astype(bf16)
    before = (iota((n_own, n_own), 0) < iota((n_own, n_own), 1)).astype(bf16)
    seen = dot(owner_b, before, 1, 0)
    slot = jnp.sum(jnp.where(owner_hot, seen, 0.0), axis=0, keepdims=True).astype(i32)
    at_slot = iota((slots, n_own), 0) == slot + r * cap
    high = (row >> 4) + 1
    low = (row & 15) * 16 + lane // cand
    req = dot(owner_b, jnp.where(at_slot, high, 0).astype(bf16), 1, 1) * 256.0 + dot(
        owner_b, jnp.where(at_slot, low, 0).astype(bf16), 1, 1
    )
    q_all = lax.all_gather(query_embed[0], "group", axis=0, tiled=True)
    got = lax.all_to_all(req, ("group", "pair"), split_axis=0, concat_axis=0, tiled=True)
    packed = got.reshape(n_group, n_pair, slots).sum(1).reshape(1, n_group * slots).astype(i32)
    pq = dot(q_all, projection, 1, 1).astype(bf16)
    s_t = dot(pq, passage_hidden, 1, 1) * inv_root
    s_hi, s_lo = halves(s_t)
    place = (iota((rows, n_group * slots), 0) == (packed >> 4) - 16).astype(bf16)
    z = dot(s_hi, place, 1, 0) + dot(s_lo, place, 1, 0)
    slot_query = (packed & 15) + q_rows * (iota((1, n_group * slots), 1) // slots)
    slot_score = jnp.sum(
        jnp.where(iota((queries_n, n_group * slots), 0) == slot_query, z, 0.0), axis=0
    ).reshape(n_group, 1, slots)
    to_send = jnp.broadcast_to(slot_score, (n_group, n_pair, slots)).reshape(n_dev, slots)
    table = lax.all_to_all(to_send, ("group", "pair"), split_axis=0, concat_axis=0, tiled=True)
    tags = (owner * cap + slot).reshape(q_rows, cand)
    tags_k = lax.all_to_all(tags, "pair", split_axis=0, concat_axis=0, tiled=True).reshape(1, k_all)
    teach_k = lax.all_to_all(
        teacher_scores.reshape(q_rows, cand), "pair", split_axis=0, concat_axis=0, tiled=True
    ).reshape(1, k_all)
    k_owner = (iota((n_dev, k_all), 0) == tags_k // cap).astype(bf16)
    k_slot = (iota((slots, k_all), 0) == tags_k % cap + cap * (iota((1, k_all), 1) // cand)).astype(f32)
    t_hi, t_lo = halves(table.T)
    picked = dot(t_hi, k_owner, 1, 0) + dot(t_lo, k_owner, 1, 0)
    s_k = jnp.sum(picked * k_slot, axis=0, keepdims=True)
    tanh_s = jnp.tanh(s_k.T - s_k)
    tanh_t = jnp.tanh(teach_k.T - teach_k)
    gap = 0.5 * (jnp.sum(tanh_s, 0, keepdims=True) - jnp.sum(tanh_t, 0, keepdims=True))
    loss = 6.0 * jnp.sum(gap * gap, axis=1, keepdims=True) / den
    grad = loss_scale * 12.0 * gap / den
    s_grad = 0.5 * jnp.sum((grad.T - grad) * (1.0 - tanh_s * tanh_s), axis=0, keepdims=True)
    values = dot(k_owner, (k_slot * s_grad).astype(bf16), 1, 1)
    back = lax.all_to_all(values, ("group", "pair"), split_axis=0, concat_axis=0, tiled=True)
    same_group = iota((queries_n, n_group * slots), 0) // q_rows == iota((queries_n, n_group * slots), 1) // slots
    spread = jnp.where(same_group, jnp.tile(back, (1, n_group)), 0.0).astype(bf16)
    w_t = dot(place, spread, 1, 1).astype(bf16)
    hidden_grad = (dot(w_t, pq, 1, 0) * inv_root).astype(bf16)
    u_part = dot(w_t, passage_hidden, 0, 0).astype(bf16)
    u_rows = lax.all_to_all(u_part, ("group", "pair"), split_axis=0, concat_axis=0, tiled=True)
    u_cols = lax.all_to_all(u_part.T, ("group", "pair"), split_axis=0, concat_axis=0, tiled=True)
    u_row = jnp.sum(u_rows.astype(f32), 0, keepdims=True) * inv_root
    u_col = jnp.sum(u_cols.astype(f32).reshape(n_dev, width // n_dev, queries_n), 0) * inv_root
    r_hi, r_lo = halves(u_row)
    c_hi, c_lo = halves(u_col)
    query_grad = dot(r_hi, projection, 1, 0) + dot(r_lo, projection, 1, 0)
    projection_grad = dot(c_hi, q_all, 1, 0) + dot(c_lo, q_all, 1, 0)
    return loss, query_grad.reshape(1, 1, width), hidden_grad, projection_grad


def solution(mesh):
    placed = (
        P("group", None, None),
        P("group", "pair", None, None),
        P("group", "pair", None, None, None),
        P("group", "pair", None, None),
        P(("group", "pair"), None),
        P(),
    )
    return jax.shard_map(
        shards,
        mesh=mesh,
        in_specs=placed,
        out_specs=(
            P("group", "pair"),
            P("group", "pair", None),
            P(("group", "pair"), None),
            P(("group", "pair"), None),
        ),
        check_vma=False,
    )
```

time: 968 us -> 142 us (0.15)
  the two profiles are of different devices: /device:TPU:0 before, /device:TPU:1 now
where the time goes in v1:
time: 142 us
  waiting for transfers between devices  46.8 us (33%)
  starting transfers between devices  39.6 us (28%)
  matrix products  20.5 us (14%)
  blocking collectives  15 us (11%)
  other arithmetic  9 us (6%)
  local copies, waits for them, and re-layouts  8.09 us (6%)
  between operations  2.65 us (2%)
    dot_general x17, matrix products, dot(): lax.dot_general(a, b, (((ca,), (cb,)), ((), ())), preferred_element_type=...  20.5 us
    all_gather x1, blocking collectives, shards(): q_all = lax.all_gather(query_embed[0], 'group', axis=0, tiled=True)  15 us
    all_to_all x1, waiting for transfers between devices, shards(): lax.all_to_all(to_send, ('group', 'pair'), split_axis=0, concat_axis=0, t...  9.29 us
    all_to_all x1, waiting for transfers between devices, shards(): lax.all_to_all(values, ('group', 'pair'), split_axis=0, concat_axis=0, ti...  8.86 us
    all_to_all x1, waiting for transfers between devices, shards(): lax.all_to_all(req, ('group', 'pair'), split_axis=0, concat_axis=0, tiled...  8.3 us
    all_to_all x1, waiting for transfers between devices, shards(): lax.all_to_all(u_part.T, ('group', 'pair'), split_axis=0, concat_axis=0,...  7.87 us
    all_to_all x1, starting transfers between devices, shards(): lax.all_to_all(tags, 'pair', split_axis=0, concat_axis=0, tiled=True)  7.58 us
    all_to_all x1, waiting for transfers between devices, shards(): lax.all_to_all(u_part, ('group', 'pair'), split_axis=0, concat_axis=0, ti...  6.95 us
  transfers between devices with their start and end apart: 7, of which 6 were waited for; matrix products, arithmetic and copies ran while one was open for 12% of the time, Pallas kernels for 0%

profile of v1, /device:TPU:1, one launch (start us, length us, event | category | flops | bytes accessed | tf_op | source)
XLA Modules:
  0.0 141.7 jit_solution(1238981770986733830)
XLA Ops:
  0.6 0.8 broadcast_multiply_fusion
  1.5 0.5 broadcast.374
  2.0 1.4 reduce.11
  3.5 0.3 fusion.12
  3.8 0.6 add.119
  4.4 7.6 %all-to-all-start = ((s32[16,1,32]{2,1,0:T(1,128)}), s32[16,1,32]{2,1,0:T(1,128)S(1)}, u32[]{:S(2)}, u32[]{:S(2)}) async-start(s32[16,1,32]{2,1,0:T(1,128)} %add.119), calls=%async_computation | async-start | bytes 16384 | tf_op jit(solution)/shard_map/all_to_all | solution.py:69
  12.0 0.7 and_multiply_fusion
  12.9 15.0 %all-gather = bf16[1,128,1024]{2,1,0:T(8,128)(2,1)S(1)} all-gather(bf16[1,16,1024]{2,1,0:T(8,128)(2,1)} %param.6), channel_id=2, replica_groups=mesh['group'=8,'pair'=16] {'group'}, dimensions={1}, use_global_device_ids=true | all-gather | bytes 294912 | tf_op jit(solution)/shard_map/all_gather | solution.py:54
  28.1 0.8 convolution_add_fusion.1
  28.9 0.8 convolution_convert_fusion
  29.8 4.7 %convolution_multiply_fusion = f32[128,2048]{1,0:T(8,128)} fusion(bf16[128,1024]{1,0:T(8,128)(2,1)S(1)} %convolution_convert_fusion, bf16[2048,1024]{1,0:T(8,128)(2,1)} %param.10), kind=kOutput, calls=%fused_computation.8 | convolution fusion | flops 537133056 | bytes 5505024 | tf_op jit(solution)/shard_map/dot_general | solution.py:17
  34.5 6.9 %all-to-all-start.3 = ((f32[16,1,32]{2,1,0:T(1,128)}), f32[16,1,32]{2,1,0:T(1,128)S(1)}, u32[]{:S(2)}, u32[]{:S(2)}) async-start(f32[16,1,32]{2,1,0:T(1,128)} %bitcast.13), calls=%async_computation.3 | async-start | bytes 16384 | tf_op jit(solution)/shard_map/all_to_all | solution.py:70
  41.4 0.7 reduce.12
  42.2 5.6 %all-to-all-done.3 = f32[16,1,32]{2,1,0:T(1,128)S(1)} async-done(((f32[16,1,32]{2,1,0:T(1,128)}), f32[16,1,32]{2,1,0:T(1,128)S(1)}, u32[]{:S(2)}, u32[]{:S(2)}) %all-to-all-start.3) | async-done | bytes 2080 | tf_op jit(solution)/shard_map/all_to_all | solution.py:70
  47.7 6.5 %all-to-all-start.1 = ((f32[128,1,128]{2,1,0:T(1,128)}), f32[128,1,128]{2,1,0:T(1,128)S(1)}, u32[]{:S(2)}, u32[]{:S(2)}) async-start(f32[128,1,128]{2,1,0:T(1,128)} %bitcast.3), calls=%async_computation.1 | async-start | bytes 131072 | tf_op jit(solution)/shard_map/all_to_all | solution.py:55
  54.3 0.5 broadcast.376
  54.8 0.7 reduce.13
  55.6 8.3 %all-to-all-done.1 = f32[128,1,128]{2,1,0:T(1,128)S(1)} async-done(((f32[128,1,128]{2,1,0:T(1,128)}), f32[128,1,128]{2,1,0:T(1,128)S(1)}, u32[]{:S(2)}, u32[]{:S(2)}) %all-to-all-start.1) | async-done | bytes 65568 | tf_op jit(solution)/shard_map/all_to_all | solution.py:55
  63.9 3.3 %fusion.1 = f32[128,1024]{1,0:T(8,128)S(1)} fusion(s32[1024]{0:T(1024)S(1)} %add_bitcast_fusion, f32[128,2048]{1,0:T(8,128)} %convolution_multiply_fusion), kind=kOutput, calls=%fused_computation.3 | convolution fusion | flops 540016640 | bytes 1576960 | tf_op jit(solution)/shard_map/dot_general | solution.py:17
  67.3 1.8 %fusion.9 = f32[1024]{0:T(1024)S(1)} fusion(f32[128,1024]{1,0:T(8,128)S(1)} %fusion.1, s32[1024]{0:T(1024)S(1)} %add_bitcast_fusion, f32[128,2048]{1,0:T(8,128)S(1)} %copy-done.2, s32[1024]{0:T(1024)S(1)} %bitcast_add_fusion), kind=kOutput, calls=%fused_computation.15 | convolution fusion | flops 539753472 | bytes 1585152 | tf_op jit(solution)/shard_map/dot_general | solution.py:17
  69.1 0.6 broadcast_in_dim.47
  69.7 4.5 %all-to-all-start.2 = ((f32[128,1,128]{2,1,0:T(1,128)}), f32[128,1,128]{2,1,0:T(1,128)S(1)}, u32[]{:S(2)}, u32[]{:S(2)}) async-start(f32[128,1,128]{2,1,0:T(1,128)} %bitcast.9), calls=%async_computation.2 | async-start | bytes 131072 | tf_op jit(solution)/shard_map/all_to_all | solution.py:67
  74.4 9.3 %all-to-all-done.2 = f32[128,1,128]{2,1,0:T(1,128)S(1)} async-done(((f32[128,1,128]{2,1,0:T(1,128)}), f32[128,1,128]{2,1,0:T(1,128)S(1)}, u32[]{:S(2)}, u32[]{:S(2)}) %all-to-all-start.2) | async-done | bytes 65568 | tf_op jit(solution)/shard_map/all_to_all | solution.py:67
  83.9 0.2 fusion.11
  84.1 0.2 fusion.13
  84.4 0.6 broadcast_multiply_fusion.1
  85.0 0.3 multiply_reduce_fusion
  85.3 0.8 fusion.24
  86.1 4.5 %all-to-all-start.4 = ((f32[128,1,128]{2,1,0:T(1,128)}), f32[128,1,128]{2,1,0:T(1,128)S(1)}, u32[]{:S(2)}, u32[]{:S(2)}) async-start(f32[128,1,128]{2,1,0:T(1,128)} %bitcast.16), calls=%async_computation.4 | async-start | bytes 131072 | tf_op jit(solution)/shard_map/all_to_all | solution.py:85
  91.3 8.9 %all-to-all-done.4 = f32[128,1,128]{2,1,0:T(1,128)S(1)} async-done(((f32[128,1,128]{2,1,0:T(1,128)}), f32[128,1,128]{2,1,0:T(1,128)S(1)}, u32[]{:S(2)}, u32[]{:S(2)}) %all-to-all-start.4) | async-done | bytes 65568 | tf_op jit(solution)/shard_map/all_to_all | solution.py:85
  100.2 1.6 %fusion.6 = bf16[2048,128]{1,0:T(8,128)(2,1)S(1)} fusion(s32[1024]{0:T(1024)S(1)} %add_bitcast_fusion, bf16[16,8,8,128]{3,2,1,0:T(8,128)(2,1)S(1)} %bitcast.62, s32[1024]{0:T(1024)S(1)} %get-tuple-element.14, s32[1024]{0:T(1024)S(1)} %get-tuple-element.15, s32[128]{0:T(128)S(1)} %get-tuple-element.16, s32[128]{0:T(128)S(1)} %get-tuple-element.17, ...), kind=kOutput, calls=%fused_computation.9 | convolution fusion | flops 539754496 | bytes 800896 | tf_op jit(solution)/shard_map/dot_general | solution.py:17
  101.8 0.5 copy-done.1
  102.3 0.8 convolution_convert_fusion.1
  103.1 0.5 broadcast.377
  103.6 1.5 %reduce.14 = bf16[128,1024]{1,0:T(8,128)(2,1)} reduce(bf16[128,1,1024]{2,0,1:T(8,128)(2,1)S(1)} %bitcast.58, bf16[]{:T(256)} %broadcast.377), dimensions={1}, to_apply=%copy.19.reduce_sub_computation | reduce | bytes 524290 | tf_op jit(solution)/shard_map/all_to_all | solution.py:91
  105.1 1.8 %reshape.398 = bf16[128,2,512]{2,1,0:T(2,128)(2,1)} reshape(bf16[128,1024]{1,0:T(8,128)(2,1)} %reduce.14) | data formatting | bytes 524288
  106.9 5.4 %all-to-all-start.5 = ((bf16[128,2,512]{2,1,0:T(2,128)(2,1)}), bf16[128,2,512]{2,1,0:T(2,128)(2,1)}, u32[]{:S(2)}, u32[]{:S(2)}) async-start(bf16[128,2,512]{2,1,0:T(2,128)(2,1)} %reshape.398), calls=%async_computation.5 | async-start | bytes 524288 | tf_op jit(solution)/shard_map/all_to_all | solution.py:91
  112.3 0.8 copy.20
  113.2 3.3 %multiply_convert_fusion = bf16[2048,1024]{1,0:T(8,128)(2,1)} fusion(bf16[2048,128]{1,0:T(8,128)(2,1)S(1)} %fusion.6, bf16[128,1024]{1,0:T(8,128)(2,1)S(1)} %convolution_convert_fusion), kind=kOutput, calls=%fused_computation | convolution fusion | flops 541065216 | bytes 4980736 | tf_op jit(solution)/shard_map/dot_general | solution.py:17
  116.4 7.0 %all-to-all-done.5 = bf16[128,2,512]{2,1,0:T(2,128)(2,1)} async-done(((bf16[128,2,512]{2,1,0:T(2,128)(2,1)}), bf16[128,2,512]{2,1,0:T(2,128)(2,1)}, u32[]{:S(2)}, u32[]{:S(2)}) %all-to-all-start.5) | async-done | bytes 262176 | tf_op jit(solution)/shard_map/all_to_all | solution.py:91
  123.4 4.2 %all-to-all-start.6 = ((bf16[128,8,128]{2,1,0:T(8,128)(2,1)}), bf16[128,8,128]{2,1,0:T(8,128)(2,1)S(1)}, u32[]{:S(2)}, u32[]{:S(2)}) async-start(bf16[128,8,128]{2,1,0:T(8,128)(2,1)} %bitcast.23), calls=%async_computation.6 | async-start | bytes 524288 | tf_op jit(solution)/shard_map/all_to_all | solution.py:92
  127.6 2.2 %reshape.399 = bf16[128,1,1024]{2,1,0:T(2,128)(2,1)S(1)} reshape(bf16[128,2,512]{2,1,0:T(2,128)(2,1)} %all-to-all-done.5) | data formatting | bytes 524288
  129.8 0.5 convert_reduce_fusion.1
  130.3 0.4 fusion.68
  130.6 0.4 fusion.67
  131.0 7.9 %all-to-all-done.6 = bf16[128,8,128]{2,1,0:T(8,128)(2,1)S(1)} async-done(((bf16[128,8,128]{2,1,0:T(8,128)(2,1)}), bf16[128,8,128]{2,1,0:T(8,128)(2,1)S(1)}, u32[]{:S(2)}, u32[]{:S(2)}) %all-to-all-start.6) | async-done | bytes 262176 | tf_op jit(solution)/shard_map/all_to_all | solution.py:92
  139.2 0.8 convolution_add_fusion.2
  140.0 0.6 add.131
  (32 shorter events, 1.5 us)
Async XLA Ops:
  0.6 28.3 %copy-start = (bf16[1024,1024]{1,0:T(8,128)(2,1)S(1)}, bf16[1024,1024]{1,0:T(8,128)(2,1)}, u32[]{:S(2)}) copy-start(bf16[1024,1024]{1,0:T(8,128)(2,1)} %param.11) | copy-start | bytes 6291460
  4.4 30.0 %all-to-all-start = ((s32[16,1,32]{2,1,0:T(1,128)}), s32[16,1,32]{2,1,0:T(1,128)S(1)}, u32[]{:S(2)}, u32[]{:S(2)}) async-start(s32[16,1,32]{2,1,0:T(1,128)} %add.119), calls=%async_computation | async-start | bytes 16384 | tf_op jit(solution)/shard_map/all_to_all | solution.py:69
  34.5 13.3 %all-to-all-start.3 = ((f32[16,1,32]{2,1,0:T(1,128)}), f32[16,1,32]{2,1,0:T(1,128)S(1)}, u32[]{:S(2)}, u32[]{:S(2)}) async-start(f32[16,1,32]{2,1,0:T(1,128)} %bitcast.13), calls=%async_computation.3 | async-start | bytes 16384 | tf_op jit(solution)/shard_map/all_to_all | solution.py:70
  47.7 16.1 %all-to-all-start.1 = ((f32[128,1,128]{2,1,0:T(1,128)}), f32[128,1,128]{2,1,0:T(1,128)S(1)}, u32[]{:S(2)}, u32[]{:S(2)}) async-start(f32[128,1,128]{2,1,0:T(1,128)} %bitcast.3), calls=%async_computation.1 | async-start | bytes 131072 | tf_op jit(solution)/shard_map/all_to_all | solution.py:55
  63.9 3.4 %copy-start.2 = (f32[128,2048]{1,0:T(8,128)S(1)}, f32[128,2048]{1,0:T(8,128)}, u32[]{:S(2)}) copy-start(f32[128,2048]{1,0:T(8,128)} %convolution_multiply_fusion) | copy-start | bytes 3145732
  69.7 14.0 %all-to-all-start.2 = ((f32[128,1,128]{2,1,0:T(1,128)}), f32[128,1,128]{2,1,0:T(1,128)S(1)}, u32[]{:S(2)}, u32[]{:S(2)}) async-start(f32[128,1,128]{2,1,0:T(1,128)} %bitcast.9), calls=%async_computation.2 | async-start | bytes 131072 | tf_op jit(solution)/shard_map/all_to_all | solution.py:67
  86.1 14.0 %all-to-all-start.4 = ((f32[128,1,128]{2,1,0:T(1,128)}), f32[128,1,128]{2,1,0:T(1,128)S(1)}, u32[]{:S(2)}, u32[]{:S(2)}) async-start(f32[128,1,128]{2,1,0:T(1,128)} %bitcast.16), calls=%async_computation.4 | async-start | bytes 131072 | tf_op jit(solution)/shard_map/all_to_all | solution.py:85
  100.2 2.2 %copy-start.1 = (bf16[2048,1024]{1,0:T(8,128)(2,1)S(1)}, bf16[2048,1024]{1,0:T(8,128)(2,1)}, u32[]{:S(2)}) copy-start(bf16[2048,1024]{1,0:T(8,128)(2,1)} %param.10) | copy-start | bytes 12582916
  106.9 16.5 %all-to-all-start.5 = ((bf16[128,2,512]{2,1,0:T(2,128)(2,1)}), bf16[128,2,512]{2,1,0:T(2,128)(2,1)}, u32[]{:S(2)}, u32[]{:S(2)}) async-start(bf16[128,2,512]{2,1,0:T(2,128)(2,1)} %reshape.398), calls=%async_computation.5 | async-start | bytes 524288 | tf_op jit(solution)/shard_map/all_to_all | solution.py:91
  123.4 15.5 %all-to-all-start.6 = ((bf16[128,8,128]{2,1,0:T(8,128)(2,1)}), bf16[128,8,128]{2,1,0:T(8,128)(2,1)S(1)}, u32[]{:S(2)}, u32[]{:S(2)}) async-start(bf16[128,8,128]{2,1,0:T(8,128)(2,1)} %bitcast.23), calls=%async_computation.6 | async-start | bytes 524288 | tf_op jit(solution)/shard_map/all_to_all | solution.py:92

commit v2 on v1

v2 whole, which is shorter than its diff:
```python
import functools
import math

import jax
import jax.numpy as jnp
from jax import lax
from jax.experimental import pallas as pl
from jax.experimental.pallas import tpu as pltpu
from jax.sharding import PartitionSpec as P

MESH = pl.DeviceIdType.MESH
loss_scale = 1024.0
f32, bf16, i32 = jnp.float32, jnp.bfloat16, jnp.int32


def iota(shape, dim):
    return lax.broadcasted_iota(i32, shape, dim)


def dot(a, b, ca, cb):
    return lax.dot_general(a, b, (((ca,), (cb,)), ((), ())), preferred_element_type=f32)


def halves(x):
    high = x.astype(bf16)
    return high, (x - high.astype(f32)).astype(bf16)


def flat_row(x):
    return jnp.concatenate([x[i : i + 1, :] for i in range(x.shape[0])], axis=1)


def step_kernel(
    n_group, n_pair, cap,
    q_ref, teach_ref, owner_ref, row_ref, hid_hbm, proj_hbm,
    wt_ref, pq_ref, loss_ref, qg_ref, pg_ref,
    hid, proj, q_all, req_out, req_in, key_out, key_in, score_out, score_in,
    value_out, value_in, place, tanh_s, u_wide, u_out, u_in,
    load_sem, send_sem, recv_sem,
):
    n_dev = n_group * n_pair
    q_rows, width = q_ref.shape
    cand = teach_ref.shape[1]
    n_own = q_rows * cand
    k_all = cand * n_pair
    slots = n_pair * cap
    rows = hid.shape[0]
    den = float(k_all * (k_all * k_all - 1))
    inv_root = 1.0 / math.sqrt(width)
    g, r = lax.axis_index("group"), lax.axis_index("pair")
    me = g * n_pair + r

    load_hid = pltpu.make_async_copy(hid_hbm, hid, load_sem.at[0])
    load_proj = pltpu.make_async_copy(proj_hbm, proj, load_sem.at[1])
    load_proj.start()
    load_hid.start()

    def peer(i):
        p = lax.rem(me + i, n_dev)
        return p, {"group": p // n_pair, "pair": lax.rem(p, n_pair)}

    barrier = pltpu.get_barrier_semaphore()

    def greet(i, carry):
        _, where = peer(i)
        pl.semaphore_signal(barrier, inc=1, device_id=where, device_id_type=MESH)
        return carry

    lax.fori_loop(1, n_dev, greet, 0)

    def send_all(number, source_of, source_me, target):
        def one(i, carry):
            p, where = peer(i)
            pltpu.make_async_remote_copy(
                src_ref=source_of(p),
                dst_ref=target.at[me],
                send_sem=send_sem.at[number],
                recv_sem=recv_sem.at[number],
                device_id=where,
                device_id_type=MESH,
            ).start()
            return carry

        lax.fori_loop(1, n_dev, one, 0)
        pltpu.make_async_copy(source_me, target.at[me], recv_sem.at[number]).start()

    def all_here(number, target):
        pltpu.make_async_copy(target, target, recv_sem.at[number]).wait()

    def all_sent(number, target, count):
        part = target.at[pl.ds(0, count)]
        pltpu.make_async_copy(part, part, send_sem.at[number]).wait()

    own, row = flat_row(owner_ref[...]), flat_row(row_ref[...])
    lane = iota((1, n_own), 1)
    hot = iota((n_dev, n_own), 0) == own
    hot_f = jnp.where(hot, 1.0, 0.0)
    hot_b = hot_f.astype(bf16)
    before = jnp.where(iota((n_own, n_own), 0) < iota((n_own, n_own), 1), 1.0, 0.0).astype(bf16)
    seen = dot(hot_b, before, 1, 0)
    slot = jnp.sum(hot_f * seen, axis=0, keepdims=True).astype(i32)
    at_slot = iota((slots, n_own), 0) == slot + r * cap
    high = ((row >> 4) + 1).astype(f32)
    low = ((row & 15) * 16 + lane // cand).astype(f32)
    req = dot(hot_b, jnp.where(at_slot, high, 0.0).astype(bf16), 1, 1) * 256.0 + dot(
        hot_b, jnp.where(at_slot, low, 0.0).astype(bf16), 1, 1
    )
    req_out[:, 0, :] = req
    tag = (own * cap + slot).astype(f32)
    for q in range(q_rows):
        key_out[q, :, 0:cand] = tag[:, q * cand : (q + 1) * cand]
        key_out[q, :, cand : 2 * cand] = teach_ref[q : q + 1, :]

    pl.semaphore_wait(barrier, n_dev - 1)

    def send_q(i, carry):
        other = lax.rem(g + i, n_group)
        pltpu.make_async_remote_copy(
            src_ref=q_ref,
            dst_ref=q_all.at[g],
            send_sem=send_sem.at[0],
            recv_sem=recv_sem.at[0],
            device_id={"group": other, "pair": r},
            device_id_type=MESH,
        ).start()
        return carry

    lax.fori_loop(1, n_group, send_q, 0)
    pltpu.make_async_copy(q_ref, q_all.at[g], recv_sem.at[0]).start()
    send_all(1, lambda p: req_out.at[p], req_out.at[me], req_in)

    def send_key(i, carry):
        other = lax.rem(r + i, n_pair)
        pltpu.make_async_remote_copy(
            src_ref=key_out.at[other],
            dst_ref=key_in.at[r],
            send_sem=send_sem.at[2],
            recv_sem=recv_sem.at[2],
            device_id={"group": g, "pair": other},
            device_id_type=MESH,
        ).start()
        return carry

    lax.fori_loop(1, n_pair, send_key, 0)
    pltpu.make_async_copy(key_out.at[r], key_in.at[r], recv_sem.at[2]).start()

    all_here(0, q_all)
    load_proj.wait()
    queries_n = n_group * q_rows
    q_flat = q_all[...].reshape(queries_n, width)
    pq = dot(q_flat, proj[...], 1, 1).astype(bf16)
    pq_ref[...] = pq
    load_hid.wait()
    s_t = (dot(hid[...], pq, 1, 1) * inv_root).T
    s_hi, s_lo = halves(s_t)

    all_here(1, req_in)
    packed = jnp.sum(req_in[...].reshape(n_group, n_pair, 1, slots), axis=1).astype(i32)
    span = 2
    for h in range(n_group // span):
        rows_of = [packed[h * span + i] for i in range(span)]
        here = jnp.concatenate(rows_of, axis=1)
        mark = jnp.where(iota((rows, span * slots), 0) == (here >> 4) - 16, 1.0, 0.0).astype(bf16)
        place[:, h * span * slots : (h + 1) * span * slots] = mark
        lo_q, hi_q = h * span * q_rows, (h + 1) * span * q_rows
        z = dot(jnp.concatenate([s_hi[lo_q:hi_q], s_lo[lo_q:hi_q]], axis=0), mark, 1, 0)
        z = z[: span * q_rows] + z[span * q_rows :]
        of_query = (here & 15) + q_rows * (iota((1, span * slots), 1) // slots)
        value = jnp.sum(
            jnp.where(iota((span * q_rows, span * slots), 0) == of_query, z, 0.0), axis=0, keepdims=True
        )
        for i in range(span):
            score_out[h * span + i] = value[:, i * slots : (i + 1) * slots]
    send_all(3, lambda p: score_out.at[p // n_pair], score_out.at[g], score_in)

    all_here(2, key_in)
    keys = key_in[:, 0, :]
    tags = flat_row(keys[:, 0:cand]).astype(i32)
    teach = flat_row(keys[:, cand : 2 * cand])
    k_owner = jnp.where(iota((n_dev, k_all), 0) == tags // cap, 1.0, 0.0).astype(bf16)
    k_slot = jnp.where(
        iota((slots, k_all), 0) == tags % cap + cap * (iota((1, k_all), 1) // cand), 1.0, 0.0
    )

    def column(x):
        return jnp.broadcast_to(x, (128, k_all)).T

    blocks = [(j * 128, (j + 1) * 128) for j in range(k_all // 128)]
    t_col = column(teach)
    t_sum = jnp.concatenate(
        [jnp.sum(jnp.tanh(t_col - teach[:, a:b]), axis=0, keepdims=True) for a, b in blocks], axis=1
    )
    all_here(3, score_in)
    t_hi, t_lo = halves(score_in[:, 0, :].T)
    picked = dot(jnp.concatenate([t_hi, t_lo], axis=0), k_owner, 1, 0)
    s_k = jnp.sum((picked[:slots] + picked[slots:]) * k_slot, axis=0, keepdims=True)
    s_col = column(s_k)
    sums = []
    for a, b in blocks:
        soft = jnp.tanh(s_col - s_k[:, a:b])
        tanh_s[:, a:b] = soft
        sums.append(jnp.sum(soft, axis=0, keepdims=True))
    gap = 0.5 * (jnp.concatenate(sums, axis=1) - t_sum)
    loss_ref[...] = 6.0 * jnp.sum(gap * gap, axis=1, keepdims=True) / den
    grad = gap * (loss_scale * 12.0 / den)
    g_col = column(grad)
    parts = []
    for a, b in blocks:
        soft = tanh_s[:, a:b]
        parts.append(
            jnp.sum((g_col - grad[:, a:b]) * (1.0 - soft * soft), axis=0, keepdims=True)
        )
    s_grad = 0.5 * jnp.concatenate(parts, axis=1)
    value_out[:, 0, :] = dot(k_owner, (k_slot * s_grad).astype(bf16), 1, 1)
    send_all(4, lambda p: value_out.at[p], value_out.at[me], value_in)

    all_here(4, value_in)
    back = value_in[:, 0, :]
    spread = jnp.concatenate(
        [jnp.where(iota((n_dev, slots), 0) // n_pair == h, back, 0.0) for h in range(n_group)], axis=1
    ).astype(bf16)
    w_t = dot(place[...], spread, 1, 1).astype(bf16)
    wt_ref[...] = w_t
    u = dot(w_t, hid[...], 0, 0)
    per = width // n_dev
    for b in range(width // 128):
        u_wide[:, b, :] = u[:, b * 128 : (b + 1) * 128]
    u_wide[:, width // 128 :, :] = u.T.reshape(n_dev, per, 128)
    u_out[...] = u_wide[...].astype(bf16)
    send_all(5, lambda p: u_out.at[p], u_out.at[me], u_in)
    all_here(5, u_in)
    total = jnp.sum(u_in[...].astype(f32), axis=0) * inv_root
    n_b = width // 128
    u_row, u_col = total[:n_b], total[n_b:]
    wide = jnp.concatenate(
        [jnp.where(iota((n_b, 128), 0) == b, u_row, 0.0) for b in range(n_b)], axis=1
    )
    w_hi, w_lo = halves(wide)
    query_grad = dot(jnp.concatenate([w_hi, w_lo], axis=0), proj[...], 1, 0)
    qg_ref[...] = jnp.sum(query_grad, axis=0, keepdims=True)
    c_hi, c_lo = halves(u_col)
    proj_grad = dot(jnp.concatenate([c_hi, c_lo], axis=0), q_flat, 1, 0)
    pg_ref[...] = proj_grad[:per] + proj_grad[per:]

    part = q_all.at[pl.ds(0, n_group - 1)]
    pltpu.make_async_copy(part, part, send_sem.at[0]).wait()
    all_sent(1, req_in, n_dev - 1)
    all_sent(2, key_in, n_pair - 1)
    all_sent(3, score_in, n_dev - 1)
    all_sent(4, value_in, n_dev - 1)
    all_sent(5, u_in, n_dev - 1)


def finish_kernel(inv_root, wt_ref, pq_ref, loss_ref, qg_ref, pg_ref, hg_out, loss_out, qg_out, pg_out):
    hg_out[...] = (dot(wt_ref[...], pq_ref[...], 1, 0) * inv_root).astype(bf16)

    @pl.when(pl.program_id(0) == 0)
    def _():
        loss_out[...] = loss_ref[...]
        qg_out[...] = qg_ref[...]
        pg_out[...] = pg_ref[...]


def shards(query_embed, teacher_scores, pair_owner, pair_row, passage_hidden, projection):
    width = query_embed.shape[2]
    q_rows = query_embed.shape[1]
    cand = teacher_scores.shape[3]
    n_pair, n_group = lax.axis_size("pair"), lax.axis_size("group")
    n_dev = n_pair * n_group
    cap = max(2, 2 * q_rows * cand // n_dev)
    slots = n_pair * cap
    k_all = cand * n_pair
    queries_n = n_group * q_rows
    rows = passage_hidden.shape[0]
    per = width // n_dev
    vmem = pl.BlockSpec(memory_space=pltpu.VMEM)
    hbm = pl.BlockSpec(memory_space=pl.ANY)
    message = pltpu.VMEM((n_dev, 1, slots), f32)
    w_t, pq, loss, query_grad, projection_grad = pl.pallas_call(
        functools.partial(step_kernel, n_group, n_pair, cap),
        out_shape=(
            jax.ShapeDtypeStruct((rows, queries_n), bf16),
            jax.ShapeDtypeStruct((queries_n, width), bf16),
            jax.ShapeDtypeStruct((1, 1), f32),
            jax.ShapeDtypeStruct((1, width), f32),
            jax.ShapeDtypeStruct((per, width), f32),
        ),
        in_specs=[vmem, vmem, vmem, vmem, hbm, hbm],
        out_specs=(vmem,) * 5,
        scratch_shapes=[
            pltpu.VMEM((rows, width), bf16),
            pltpu.VMEM((width, width), bf16),
            pltpu.VMEM((n_group, q_rows, width), bf16),
            message,
            message,
            pltpu.VMEM((q_rows, 1, 128), f32),
            pltpu.VMEM((n_pair, 1, 128), f32),
            pltpu.VMEM((n_group, 1, slots), f32),
            message,
            message,
            message,
            pltpu.VMEM((rows, n_group * slots), bf16),
            pltpu.VMEM((k_all, k_all), f32),
            pltpu.VMEM((n_dev, 16, 128), f32),
            pltpu.VMEM((n_dev, 16, 128), bf16),
            pltpu.VMEM((n_dev, 16, 128), bf16),
            pltpu.SemaphoreType.DMA((2,)),
            pltpu.SemaphoreType.DMA((6,)),
            pltpu.SemaphoreType.DMA((6,)),
        ],
        compiler_params=pltpu.CompilerParams(collective_id=0, has_side_effects=True),
        name="step",
    )(
        query_embed[0],
        teacher_scores.reshape(q_rows, cand),
        pair_owner.reshape(q_rows, cand),
        pair_row.reshape(q_rows, cand),
        passage_hidden,
        projection,
    )
    tile = 512

    def whole(shape):
        return pl.BlockSpec(shape, lambda i: (0, 0))

    hidden_grad, loss, query_grad, projection_grad = pl.pallas_call(
        functools.partial(finish_kernel, 1.0 / math.sqrt(width)),
        grid=(rows // tile,),
        out_shape=(
            jax.ShapeDtypeStruct((rows, width), bf16),
            jax.ShapeDtypeStruct((1, 1), f32),
            jax.ShapeDtypeStruct((1, width), f32),
            jax.ShapeDtypeStruct((per, width), f32),
        ),
        in_specs=[
            pl.BlockSpec((tile, queries_n), lambda i: (i, 0)),
            whole((queries_n, width)),
            whole((1, 1)),
            whole((1, width)),
            whole((per, width)),
        ],
        out_specs=(
            pl.BlockSpec((tile, width), lambda i: (i, 0)),
            whole((1, 1)),
            whole((1, width)),
            whole((per, width)),
        ),
        name="finish",
    )(w_t, pq, loss, query_grad, projection_grad)
    return loss, query_grad.reshape(1, 1, width), hidden_grad, projection_grad


def solution(mesh):
    placed = (
        P("group", None, None),
        P("group", "pair", None, None),
        P("group", "pair", None, None, None),
        P("group", "pair", None, None),
        P(("group", "pair"), None),
        P(),
    )
    return jax.shard_map(
        shards,
        mesh=mesh,
        in_specs=placed,
        out_specs=(
            P("group", "pair"),
            P("group", "pair", None),
            P(("group", "pair"), None),
            P(("group", "pair"), None),
        ),
        check_vma=False,
    )
```

time: 142 us -> 59.4 us (0.42)
  Pallas kernels: 0 us -> 58.5 us
  waiting for transfers between devices: 46.8 us -> 0 us
  starting transfers between devices: 39.6 us -> 0 us
  matrix products: 20.5 us -> 0 us
  blocking collectives: 15 us -> 0 us
  other arithmetic: 9 us -> 0 us
  local copies, waits for them, and re-layouts: 8.09 us -> 0 us
  between operations: 2.65 us -> 0.64 us
    pallas_call x0 -> x2, Pallas kernels: none -> 58.5 us  [the longest x1 53.1 us: shards(): pl.pallas_call(functools.partial(step_kernel, n_group, n_pair, cap), out_...]
    all_to_all x7 -> x0, waiting for transfers between devices: 46.8 us -> none  [the longest x1 9.29 us: shards(): lax.all_to_all(to_send, ('group', 'pair'), split_axis=0, concat_axis=0, t...]
    all_to_all x7 -> x0, starting transfers between devices: 39.6 us -> none  [the longest x1 7.58 us: shards(): lax.all_to_all(tags, 'pair', split_axis=0, concat_axis=0, tiled=True)]
    dot_general x17 -> x0, matrix products: 20.5 us -> none  [dot(): lax.dot_general(a, b, (((ca,), (cb,)), ((), ())), preferred_element_type=...]
    all_gather x1 -> x0, blocking collectives: 15 us -> none  [shards(): q_all = lax.all_gather(query_embed[0], 'group', axis=0, tiled=True)]
    unnamed x9 -> x0, local copies, waits for them, and re-layouts: 5.06 us -> none
    all_to_all x3 -> x0, other arithmetic: 2.79 us -> none  [the longest x1 1.45 us: shards(): lax.all_to_all(u_part, ('group', 'pair'), split_axis=0, concat_axis=0, ti...]
    mul x3 -> x0, other arithmetic: 1.56 us -> none  [the longest x1 0.85 us: shards(): tags = (owner * cap + slot).reshape(q_rows, cand)]
  transfers between devices with their start and end apart: 7 -> 0, of which waited for: 6 -> 0; matrix products, arithmetic and copies ran while one was open for 12% -> 0% of each run, Pallas kernels for 0% -> 0%
where the time goes in v2:
time: 59.4 us; the launch traced here: 59.1 us
  Pallas kernels  58.5 us (98%)
  between operations  0.64 us (1%)
    pallas_call x1, Pallas kernels, shards(): pl.pallas_call(functools.partial(step_kernel, n_group, n_pair, cap), out_...  53.1 us
    pallas_call x1, Pallas kernels, shards(): pl.pallas_call(functools.partial(finish_kernel, 1.0 / math.sqrt(width)),...  5.37 us

profile of v2, /device:TPU:1, one launch (start us, length us, event | category | flops | bytes accessed | tf_op | source)
XLA Modules:
  0.0 59.1 jit_solution(15644166521210175485)
XLA Ops:
  0.6 53.1 %step.1 = (bf16[2048,128]{1,0:T(8,128)(2,1)}, bf16[128,1024]{1,0:T(8,128)(2,1)}, f32[1,1]{1,0:T(1,128)}, f32[1,1024]{1,0:T(1,128)}, f32[8,1024]{1,0:T(8,128)}) custom-call(bf16[16,1024]{1,0:T(8,128)(2,1)} %bitcast.5, f32[16,32]{1,0:T(8,128)} %bitcast.6, s32[16,32]{1,0:T(8,128)} %bitcast.7, s32[16,32]{1,0:T(8,128)} %bitcast.8, bf16[2048,1024]{1,0:T(8,128)(2,1)} %hid_hbm.1, ...), custom_call_target="tpu_custom_call" | custom-call | tf_op jit(solution)/shard_map/step/pallas_call | solution.py:279
  53.8 5.4 %finish.1 = (bf16[2048,1024]{1,0:T(8,128)(2,1)}, f32[1,1]{1,0:T(1,128)}, f32[1,1024]{1,0:T(1,128)}, f32[8,1024]{1,0:T(8,128)}) custom-call(bf16[2048,128]{1,0:T(8,128)(2,1)} %get-tuple-element.13.wt_ref, bf16[128,1024]{1,0:T(8,128)(2,1)} %get-tuple-element.14.pq_ref, f32[1,1]{1,0:T(1,128)} %get-tuple-element.15.loss_ref, ...), custom_call_target="tpu_custom_call" | custom-call | tf_op jit(solution)/shard_map/finish/pallas_call | solution.py:326

commit v3 on v2

--- a/solution.py
+++ b/solution.py
@@ -32,8 +32,9 @@
 
 def step_kernel(
     n_group, n_pair, cap,
-    q_ref, teach_ref, owner_ref, row_ref, hid_hbm, proj_hbm,
-    wt_ref, pq_ref, loss_ref, qg_ref, pg_ref,
+    q_hbm, teach_hbm, owner_hbm, row_hbm, hid_hbm, proj_hbm,
+    hg_ref, loss_ref, qg_ref, pg_ref,
+    q_ref, teach_ref, owner_ref, row_ref,
     hid, proj, q_all, req_out, req_in, key_out, key_in, score_out, score_in,
     value_out, value_in, place, tanh_s, u_wide, u_out, u_in,
     load_sem, send_sem, recv_sem,
@@ -50,39 +51,52 @@
     g, r = lax.axis_index("group"), lax.axis_index("pair")
     me = g * n_pair + r
 
-    load_hid = pltpu.make_async_copy(hid_hbm, hid, load_sem.at[0])
-    load_proj = pltpu.make_async_copy(proj_hbm, proj, load_sem.at[1])
-    load_proj.start()
-    load_hid.start()
-
-    def peer(i):
-        p = lax.rem(me + i, n_dev)
-        return p, {"group": p // n_pair, "pair": lax.rem(p, n_pair)}
+    loads = [
+        pltpu.make_async_copy(source, target, load_sem.at[n])
+        for n, (source, target) in enumerate(
+            [(owner_hbm, owner_ref), (row_hbm, row_ref), (teach_hbm, teach_ref), (q_hbm, q_ref),
+             (proj_hbm, proj), (hid_hbm, hid)]
+        )
+    ]
+    for load in loads:
+        load.start()
+
+    def others(visit):
+        def ring(i, carry):
+            group = lax.rem(g + i, n_group)
+            for pair in range(n_pair):
+                visit(group, pair)
+            return carry
+
+        def row_of_pairs(i, carry):
+            visit(g, lax.rem(r + i, n_pair))
+            return carry
+
+        lax.fori_loop(1, n_group, ring, 0)
+        lax.fori_loop(1, n_pair, row_of_pairs, 0, unroll=True)
 
     barrier = pltpu.get_barrier_semaphore()
 
-    def greet(i, carry):
-        _, where = peer(i)
-        pl.semaphore_signal(barrier, inc=1, device_id=where, device_id_type=MESH)
-        return carry
-
-    lax.fori_loop(1, n_dev, greet, 0)
-
-    def send_all(number, source_of, source_me, target):
-        def one(i, carry):
-            p, where = peer(i)
+    def greet(group, pair):
+        pl.semaphore_signal(
+            barrier, inc=1, device_id={"group": group, "pair": pair}, device_id_type=MESH
+        )
+
+    others(greet)
+
+    def send_all(number, source_of, target):
+        def one(group, pair):
             pltpu.make_async_remote_copy(
-                src_ref=source_of(p),
+                src_ref=source_of(group, pair),
                 dst_ref=target.at[me],
                 send_sem=send_sem.at[number],
                 recv_sem=recv_sem.at[number],
-                device_id=where,
+                device_id={"group": group, "pair": pair},
                 device_id_type=MESH,
             ).start()
-            return carry
-
-        lax.fori_loop(1, n_dev, one, 0)
-        pltpu.make_async_copy(source_me, target.at[me], recv_sem.at[number]).start()
+
+        pltpu.make_async_copy(source_of(g, r), target.at[me], recv_sem.at[number]).start()
+        others(one)
 
     def all_here(number, target):
         pltpu.make_async_copy(target, target, recv_sem.at[number]).wait()
@@ -91,6 +105,8 @@
         part = target.at[pl.ds(0, count)]
         pltpu.make_async_copy(part, part, send_sem.at[number]).wait()
 
+    for load in loads[:3]:
+        load.wait()
     own, row = flat_row(owner_ref[...]), flat_row(row_ref[...])
     lane = iota((1, n_own), 1)
     hot = iota((n_dev, n_own), 0) == own
@@ -111,6 +127,7 @@
         key_out[q, :, 0:cand] = tag[:, q * cand : (q + 1) * cand]
         key_out[q, :, cand : 2 * cand] = teach_ref[q : q + 1, :]
 
+    loads[3].wait()
     pl.semaphore_wait(barrier, n_dev - 1)
 
     def send_q(i, carry):
@@ -125,9 +142,9 @@
         ).start()
         return carry
 
-    lax.fori_loop(1, n_group, send_q, 0)
+    lax.fori_loop(1, n_group, send_q, 0, unroll=True)
     pltpu.make_async_copy(q_ref, q_all.at[g], recv_sem.at[0]).start()
-    send_all(1, lambda p: req_out.at[p], req_out.at[me], req_in)
+    send_all(1, lambda group, pair: req_out.at[group * n_pair + pair], req_in)
 
     def send_key(i, carry):
         other = lax.rem(r + i, n_pair)
@@ -141,17 +158,16 @@
         ).start()
         return carry
 
-    lax.fori_loop(1, n_pair, send_key, 0)
+    lax.fori_loop(1, n_pair, send_key, 0, unroll=True)
     pltpu.make_async_copy(key_out.at[r], key_in.at[r], recv_sem.at[2]).start()
 
     all_here(0, q_all)
-    load_proj.wait()
+    loads[4].wait()
     queries_n = n_group * q_rows
     q_flat = q_all[...].reshape(queries_n, width)
-    pq = dot(q_flat, proj[...], 1, 1).astype(bf16)
-    pq_ref[...] = pq
-    load_hid.wait()
-    s_t = (dot(hid[...], pq, 1, 1) * inv_root).T
+    pq = (dot(q_flat, proj[...], 1, 1) * inv_root).astype(bf16)
+    loads[5].wait()
+    s_t = dot(hid[...], pq, 1, 1).T
     s_hi, s_lo = halves(s_t)
 
     all_here(1, req_in)
@@ -171,7 +187,7 @@
         )
         for i in range(span):
             score_out[h * span + i] = value[:, i * slots : (i + 1) * slots]
-    send_all(3, lambda p: score_out.at[p // n_pair], score_out.at[g], score_in)
+    send_all(3, lambda group, pair: score_out.at[group], score_in)
 
     all_here(2, key_in)
     keys = key_in[:, 0, :]
@@ -201,7 +217,7 @@
         tanh_s[:, a:b] = soft
         sums.append(jnp.sum(soft, axis=0, keepdims=True))
     gap = 0.5 * (jnp.concatenate(sums, axis=1) - t_sum)
-    loss_ref[...] = 6.0 * jnp.sum(gap * gap, axis=1, keepdims=True) / den
+    loss_ref[...] = jnp.broadcast_to(6.0 * jnp.sum(gap * gap, axis=1, keepdims=True) / den, (1, 128))
     grad = gap * (loss_scale * 12.0 / den)
     g_col = column(grad)
     parts = []
@@ -212,7 +228,7 @@
         )
     s_grad = 0.5 * jnp.concatenate(parts, axis=1)
     value_out[:, 0, :] = dot(k_owner, (k_slot * s_grad).astype(bf16), 1, 1)
-    send_all(4, lambda p: value_out.at[p], value_out.at[me], value_in)
+    send_all(4, lambda group, pair: value_out.at[group * n_pair + pair], value_in)
 
     all_here(4, value_in)
     back = value_in[:, 0, :]
@@ -220,14 +236,16 @@
         [jnp.where(iota((n_dev, slots), 0) // n_pair == h, back, 0.0) for h in range(n_group)], axis=1
     ).astype(bf16)
     w_t = dot(place[...], spread, 1, 1).astype(bf16)
-    wt_ref[...] = w_t
     u = dot(w_t, hid[...], 0, 0)
     per = width // n_dev
     for b in range(width // 128):
         u_wide[:, b, :] = u[:, b * 128 : (b + 1) * 128]
     u_wide[:, width // 128 :, :] = u.T.reshape(n_dev, per, 128)
     u_out[...] = u_wide[...].astype(bf16)
-    send_all(5, lambda p: u_out.at[p], u_out.at[me], u_in)
+    send_all(5, lambda group, pair: u_out.at[group * n_pair + pair], u_in)
+    tile = 256
+    for i in range(rows // tile):
+        hg_ref[i * tile : (i + 1) * tile, :] = dot(w_t[i * tile : (i + 1) * tile], pq, 1, 0).astype(bf16)
     all_here(5, u_in)
     total = jnp.sum(u_in[...].astype(f32), axis=0) * inv_root
     n_b = width // 128
@@ -251,14 +269,22 @@
     all_sent(5, u_in, n_dev - 1)
 
 
-def finish_kernel(inv_root, wt_ref, pq_ref, loss_ref, qg_ref, pg_ref, hg_out, loss_out, qg_out, pg_out):
-    hg_out[...] = (dot(wt_ref[...], pq_ref[...], 1, 0) * inv_root).astype(bf16)
-
-    @pl.when(pl.program_id(0) == 0)
-    def _():
-        loss_out[...] = loss_ref[...]
-        qg_out[...] = qg_ref[...]
-        pg_out[...] = pg_ref[...]
+def finish_kernel(parts, hg_ref, loss_ref, qg_ref, pg_ref, hg_out, loss_out, qg_out, pg_out, loss_one, sem):
+    loss_one[...] = loss_ref[:, 0:1]
+    tile = hg_ref.shape[0] // parts
+    stores = [
+        pltpu.make_async_copy(source, target, sem.at[parts + n])
+        for n, (source, target) in enumerate([(loss_one, loss_out), (qg_ref, qg_out), (pg_ref, pg_out)])
+    ] + [
+        pltpu.make_async_copy(
+            hg_ref.at[pl.ds(i * tile, tile)], hg_out.at[pl.ds(i * tile, tile)], sem.at[i]
+        )
+        for i in range(parts)
+    ]
+    for store in stores:
+        store.start()
+    for store in stores:
+        store.wait()
 
 
 def shards(query_embed, teacher_scores, pair_owner, pair_row, passage_hidden, projection):
@@ -274,20 +300,23 @@
     rows = passage_hidden.shape[0]
     per = width // n_dev
     vmem = pl.BlockSpec(memory_space=pltpu.VMEM)
-    hbm = pl.BlockSpec(memory_space=pl.ANY)
+    hbm = pl.BlockSpec(memory_space=pltpu.HBM)
     message = pltpu.VMEM((n_dev, 1, slots), f32)
-    w_t, pq, loss, query_grad, projection_grad = pl.pallas_call(
+    results = pl.pallas_call(
         functools.partial(step_kernel, n_group, n_pair, cap),
         out_shape=(
-            jax.ShapeDtypeStruct((rows, queries_n), bf16),
-            jax.ShapeDtypeStruct((queries_n, width), bf16),
-            jax.ShapeDtypeStruct((1, 1), f32),
-            jax.ShapeDtypeStruct((1, width), f32),
-            jax.ShapeDtypeStruct((per, width), f32),
+            pltpu.VMEM((rows, width), bf16),
+            pltpu.VMEM((1, 128), f32),
+            pltpu.VMEM((1, width), f32),
+            pltpu.VMEM((per, width), f32),
         ),
-        in_specs=[vmem, vmem, vmem, vmem, hbm, hbm],
-        out_specs=(vmem,) * 5,
+        in_specs=[hbm] * 6,
+        out_specs=(vmem,) * 4,
         scratch_shapes=[
+            pltpu.VMEM((q_rows, width), bf16),
+            pltpu.VMEM((q_rows, cand), f32),
+            pltpu.VMEM((q_rows, cand), i32),
+            pltpu.VMEM((q_rows, cand), i32),
             pltpu.VMEM((rows, width), bf16),
             pltpu.VMEM((width, width), bf16),
             pltpu.VMEM((n_group, q_rows, width), bf16),
@@ -304,49 +333,42 @@
             pltpu.VMEM((n_dev, 16, 128), f32),
             pltpu.VMEM((n_dev, 16, 128), bf16),
             pltpu.VMEM((n_dev, 16, 128), bf16),
-            pltpu.SemaphoreType.DMA((2,)),
+            pltpu.SemaphoreType.DMA((6,)),
             pltpu.SemaphoreType.DMA((6,)),
             pltpu.SemaphoreType.DMA((6,)),
         ],
-        compiler_params=pltpu.CompilerParams(collective_id=0, has_side_effects=True),
+        compiler_params=pltpu.CompilerParams(
+            collective_id=0, has_side_effects=True, vmem_limit_bytes=44 * 2**20
+        ),
         name="step",
     )(
-        query_embed[0],
-        teacher_scores.reshape(q_rows, cand),
-        pair_owner.reshape(q_rows, cand),
-        pair_row.reshape(q_rows, cand),
-        passage_hidden,
-        projection,
-    )
-    tile = 512
-
-    def whole(shape):
-        return pl.BlockSpec(shape, lambda i: (0, 0))
-
+        *(
+            pltpu.with_memory_space_constraint(x, pltpu.HBM)
+            for x in (
+                query_embed[0],
+                teacher_scores.reshape(q_rows, cand),
+                pair_owner.reshape(q_rows, cand),
+                pair_row.reshape(q_rows, cand),
+                passage_hidden,
+                projection,
+            )
+        )
+    )
+    parts = 8
     hidden_grad, loss, query_grad, projection_grad = pl.pallas_call(
-        functools.partial(finish_kernel, 1.0 / math.sqrt(width)),
-        grid=(rows // tile,),
+        functools.partial(finish_kernel, parts),
         out_shape=(
             jax.ShapeDtypeStruct((rows, width), bf16),
             jax.ShapeDtypeStruct((1, 1), f32),
             jax.ShapeDtypeStruct((1, width), f32),
             jax.ShapeDtypeStruct((per, width), f32),
         ),
-        in_specs=[
-            pl.BlockSpec((tile, queries_n), lambda i: (i, 0)),
-            whole((queries_n, width)),
-            whole((1, 1)),
-            whole((1, width)),
-            whole((per, width)),
-        ],
-        out_specs=(
-            pl.BlockSpec((tile, width), lambda i: (i, 0)),
-            whole((1, 1)),
-            whole((1, width)),
-            whole((per, width)),
-        ),
+        in_specs=[vmem] * 4,
+        out_specs=(hbm,) * 4,
+        scratch_shapes=[pltpu.VMEM((1, 1), f32), pltpu.SemaphoreType.DMA((parts + 3,))],
+        compiler_params=pltpu.CompilerParams(vmem_limit_bytes=4 * 2**20),
         name="finish",
-    )(w_t, pq, loss, query_grad, projection_grad)
+    )(*results)
     return loss, query_grad.reshape(1, 1, width), hidden_grad, projection_grad
 
 

time: 59.4 us -> 50.2 us (0.85)
  Pallas kernels: 58.5 us -> 49.5 us
    pallas_call x1, Pallas kernels: 53.1 us -> 47.3 us  [shards(): pl.pallas_call(functools.partial(step_kernel, n_group, n_pair, cap), out_...]
    pallas_call x1, Pallas kernels: 5.37 us -> 2.12 us  [shards(): pl.pallas_call(functools.partial(finish_kernel, parts), out_shape=(jax.Sh...]
where the time goes in v3:
time: 50.2 us; the launch traced here: 50.1 us
  Pallas kernels  49.5 us (99%)
  between operations  0.64 us (1%)
    pallas_call x1, Pallas kernels, shards(): pl.pallas_call(functools.partial(step_kernel, n_group, n_pair, cap), out_...  47.3 us
    pallas_call x1, Pallas kernels, shards(): pl.pallas_call(functools.partial(finish_kernel, parts), out_shape=(jax.Sh...  2.12 us

profile of v3, /device:TPU:1, one launch (start us, length us, event | category | flops | bytes accessed | tf_op | source)
XLA Modules:
  0.0 50.1 jit_solution(5305193344454445169)
XLA Ops:
  0.6 47.3 %step.1 = (bf16[2048,1024]{1,0:T(8,128)(2,1)S(1)}, f32[1,128]{1,0:T(1,128)S(1)}, f32[1,1024]{1,0:T(1,128)S(1)}, f32[8,1024]{1,0:T(8,128)S(1)}) custom-call(bf16[16,1024]{1,0:T(8,128)(2,1)} %bitcast.5, f32[16,32]{1,0:T(8,128)} %bitcast.6, s32[16,32]{1,0:T(8,128)} %bitcast.7, s32[16,32]{1,0:T(8,128)} %bitcast.8, bf16[2048,1024]{1,0:T(8,128)(2,1)} %hid_hbm.1, ...), custom_call_target="tpu_custom_call" | custom-call | tf_op jit(solution)/shard_map/step/pallas_call | solution.py:305
  48.0 2.1 %finish.1 = (bf16[2048,1024]{1,0:T(8,128)(2,1)}, f32[1,1]{1,0:T(1,128)}, f32[1,1024]{1,0:T(1,128)}, f32[8,1024]{1,0:T(8,128)}) custom-call(bf16[2048,1024]{1,0:T(8,128)(2,1)S(1)} %get-tuple-element.12.hg_ref, f32[1,128]{1,0:T(1,128)S(1)} %get-tuple-element.13.loss_ref, f32[1,1024]{1,0:T(1,128)S(1)} %get-tuple-element.14.qg_ref, ...), custom_call_target="tpu_custom_call" | custom-call | tf_op jit(solution)/shard_map/finish/pallas_call | solution.py:358

commit v4 on v3

--- a/solution.py
+++ b/solution.py
@@ -31,13 +31,13 @@
 
 
 def step_kernel(
-    n_group, n_pair, cap,
+    n_group, n_pair, n_core, side, cap,
     q_hbm, teach_hbm, owner_hbm, row_hbm, hid_hbm, proj_hbm,
     hg_ref, loss_ref, qg_ref, pg_ref,
     q_ref, teach_ref, owner_ref, row_ref,
     hid, proj, q_all, req_out, req_in, key_out, key_in, score_out, score_in,
-    value_out, value_in, place, tanh_s, u_wide, u_out, u_in,
-    load_sem, send_sem, recv_sem,
+    value_out, value_in, place, tanh_s, s_hi, s_lo, w_ref, u_ref, u_wide, u_there, u_here, u_out, u_in,
+    load_sem, send_sem, recv_sem, plane_sem,
 ):
     n_dev = n_group * n_pair
     q_rows, width = q_ref.shape
@@ -50,6 +50,11 @@
     inv_root = 1.0 / math.sqrt(width)
     g, r = lax.axis_index("group"), lax.axis_index("pair")
     me = g * n_pair + r
+    n_plane = n_group // n_core
+    in_plane = n_core * n_pair
+    q_plane = n_core * q_rows
+    s_plane = n_core * slots
+    half = n_dev // n_core
 
     loads = [
         pltpu.make_async_copy(source, target, load_sem.at[n])
@@ -61,19 +66,34 @@
     for load in loads:
         load.start()
 
-    def others(visit):
-        def ring(i, carry):
-            group = lax.rem(g + i, n_group)
-            for pair in range(n_pair):
-                visit(group, pair)
-            return carry
-
-        def row_of_pairs(i, carry):
-            visit(g, lax.rem(r + i, n_pair))
-            return carry
-
-        lax.fori_loop(1, n_group, ring, 0)
-        lax.fori_loop(1, n_pair, row_of_pairs, 0, unroll=True)
+    z, c = g // n_core, lax.rem(g, n_core)
+    y, x = r // side, lax.rem(r, side)
+    planes = sorted(range(n_plane), key=lambda d: -min(d, n_plane - d))
+    steps = sorted(range(side), key=lambda d: -min(d, side - d))
+    near = [(dy, dx) for dy in steps for dx in steps]
+    near.sort(key=lambda d: -sum(min(v, side - v) for v in d))
+    y_at = {d: lax.rem(y + d, side) * side for d in steps}
+    x_at = {d: lax.rem(x + d, side) for d in steps}
+    pairs = [y_at[dy] + x_at[dx] for dy, dx in near]
+    z_at = {d: lax.rem(z + d, n_plane) for d in planes}
+
+    def plane_peers(dz, visit):
+        if dz:
+            def both(i, carry):
+                for pair in pairs:
+                    visit(z_at[dz] * n_core + i, pair)
+                return carry
+
+            lax.fori_loop(0, n_core, both, 0)
+        else:
+            def partners(i, carry):
+                for pair in pairs:
+                    visit(z * n_core + lax.rem(c + i, n_core), pair)
+                return carry
+
+            lax.fori_loop(1, n_core, partners, 0)
+            for pair in pairs[:-1]:
+                visit(g, pair)
 
     barrier = pltpu.get_barrier_semaphore()
 
@@ -82,21 +102,26 @@
             barrier, inc=1, device_id={"group": group, "pair": pair}, device_id_type=MESH
         )
 
-    others(greet)
-
-    def send_all(number, source_of, target):
+    for dz in planes:
+        plane_peers(dz, greet)
+
+    def send_plane(dz, send, recv, source_of, target, at):
         def one(group, pair):
             pltpu.make_async_remote_copy(
                 src_ref=source_of(group, pair),
-                dst_ref=target.at[me],
-                send_sem=send_sem.at[number],
-                recv_sem=recv_sem.at[number],
+                dst_ref=target.at[at],
+                send_sem=send,
+                recv_sem=recv,
                 device_id={"group": group, "pair": pair},
                 device_id_type=MESH,
             ).start()
 
-        pltpu.make_async_copy(source_of(g, r), target.at[me], recv_sem.at[number]).start()
-        others(one)
+        plane_peers(dz, one)
+        if dz == 0:
+            pltpu.make_async_copy(source_of(g, r), target.at[at], recv).start()
+
+    def index_of(group, pair):
+        return group * n_pair + pair
 
     def all_here(number, target):
         pltpu.make_async_copy(target, target, recv_sem.at[number]).wait()
@@ -144,7 +169,8 @@
 
     lax.fori_loop(1, n_group, send_q, 0, unroll=True)
     pltpu.make_async_copy(q_ref, q_all.at[g], recv_sem.at[0]).start()
-    send_all(1, lambda group, pair: req_out.at[group * n_pair + pair], req_in)
+    for dz in planes:
+        send_plane(dz, send_sem.at[1], recv_sem.at[1], lambda *p: req_out.at[index_of(*p)], req_in, me)
 
     def send_key(i, carry):
         other = lax.rem(r + i, n_pair)
@@ -167,27 +193,27 @@
     q_flat = q_all[...].reshape(queries_n, width)
     pq = (dot(q_flat, proj[...], 1, 1) * inv_root).astype(bf16)
     loads[5].wait()
-    s_t = dot(hid[...], pq, 1, 1).T
-    s_hi, s_lo = halves(s_t)
+    s_t = dot(pq, hid[...], 1, 1)
+    s_hi[...], s_lo[...] = halves(s_t)
 
     all_here(1, req_in)
-    packed = jnp.sum(req_in[...].reshape(n_group, n_pair, 1, slots), axis=1).astype(i32)
-    span = 2
-    for h in range(n_group // span):
-        rows_of = [packed[h * span + i] for i in range(span)]
-        here = jnp.concatenate(rows_of, axis=1)
-        mark = jnp.where(iota((rows, span * slots), 0) == (here >> 4) - 16, 1.0, 0.0).astype(bf16)
-        place[:, h * span * slots : (h + 1) * span * slots] = mark
-        lo_q, hi_q = h * span * q_rows, (h + 1) * span * q_rows
-        z = dot(jnp.concatenate([s_hi[lo_q:hi_q], s_lo[lo_q:hi_q]], axis=0), mark, 1, 0)
-        z = z[: span * q_rows] + z[span * q_rows :]
-        of_query = (here & 15) + q_rows * (iota((1, span * slots), 1) // slots)
+    of_group = iota((1, s_plane), 1) // slots
+    for n, dz in enumerate(planes):
+        asked = req_in[pl.ds(z_at[dz] * in_plane, in_plane)].reshape(n_core, n_pair, 1, slots)
+        asked = jnp.sum(asked, axis=1).astype(i32)
+        here = jnp.concatenate([asked[i] for i in range(n_core)], axis=1)
+        mark = jnp.where(iota((rows, s_plane), 0) == (here >> 4) - 16, 1.0, 0.0).astype(bf16)
+        place[n] = mark
+        of_plane = pl.ds(pl.multiple_of(z_at[dz] * q_plane, q_plane), q_plane)
+        picks = dot(jnp.concatenate([s_hi[of_plane, :], s_lo[of_plane, :]], axis=0), mark, 1, 0)
+        picks = picks[:q_plane] + picks[q_plane:]
+        of_query = (here & 15) + q_rows * of_group
         value = jnp.sum(
-            jnp.where(iota((span * q_rows, span * slots), 0) == of_query, z, 0.0), axis=0, keepdims=True
-        )
-        for i in range(span):
-            score_out[h * span + i] = value[:, i * slots : (i + 1) * slots]
-    send_all(3, lambda group, pair: score_out.at[group], score_in)
+            jnp.where(iota((q_plane, s_plane), 0) == of_query, picks, 0.0), axis=0, keepdims=True
+        )
+        for i in range(n_core):
+            score_out[z_at[dz] * n_core + i] = value[:, i * slots : (i + 1) * slots]
+        send_plane(dz, send_sem.at[3], recv_sem.at[3], lambda group, pair: score_out.at[group], score_in, me)
 
     all_here(2, key_in)
     keys = key_in[:, 0, :]
@@ -228,27 +254,72 @@
         )
     s_grad = 0.5 * jnp.concatenate(parts, axis=1)
     value_out[:, 0, :] = dot(k_owner, (k_slot * s_grad).astype(bf16), 1, 1)
-    send_all(4, lambda group, pair: value_out.at[group * n_pair + pair], value_in)
-
-    all_here(4, value_in)
-    back = value_in[:, 0, :]
-    spread = jnp.concatenate(
-        [jnp.where(iota((n_dev, slots), 0) // n_pair == h, back, 0.0) for h in range(n_group)], axis=1
-    ).astype(bf16)
-    w_t = dot(place[...], spread, 1, 1).astype(bf16)
-    u = dot(w_t, hid[...], 0, 0)
+    for dz in planes:
+        send_plane(
+            dz, send_sem.at[4], plane_sem.at[(n_plane - dz) % n_plane],
+            lambda *p: value_out.at[index_of(*p)], value_in, me,
+        )
+
+    row_of = iota((in_plane, slots), 0) // n_pair
+    for n, dz in reversed(list(enumerate(planes))):
+        arrived = value_in.at[pl.ds(z_at[dz] * in_plane, in_plane)]
+        pltpu.make_async_copy(arrived, arrived, plane_sem.at[dz]).wait()
+        back = value_in[pl.ds(z_at[dz] * in_plane, in_plane), 0, :]
+        spread = jnp.concatenate([jnp.where(row_of == i, back, 0.0) for i in range(n_core)], axis=1)
+        of_plane = pl.ds(pl.multiple_of(z_at[dz] * q_plane, q_plane), q_plane)
+        w_ref[of_plane, :] = dot(spread.astype(bf16), place[n], 1, 1).astype(bf16)
+    u_ref[...] = dot(w_ref[...], hid[...], 1, 0).reshape(n_group, q_rows, width)
     per = width // n_dev
-    for b in range(width // 128):
-        u_wide[:, b, :] = u[:, b * 128 : (b + 1) * 128]
-    u_wide[:, width // 128 :, :] = u.T.reshape(n_dev, per, 128)
-    u_out[...] = u_wide[...].astype(bf16)
-    send_all(5, lambda group, pair: u_out.at[group * n_pair + pair], u_in)
+    n_b = width // 128
+
+    def gather_half(core):
+        for plane in range(n_plane):
+            group = plane * n_core + core
+            of_rows = u_ref[group]
+            for b in range(n_b):
+                u_wide[plane * n_pair : (plane + 1) * n_pair, b, :] = of_rows[:, b * 128 : (b + 1) * 128]
+            width_group = n_pair * per
+            lanes = pl.ds(pl.multiple_of(group * width_group, width_group), width_group)
+            columns = u_ref[:, :, lanes].reshape(n_dev, width_group)
+            u_wide[plane * n_pair : (plane + 1) * n_pair, n_b:, :] = columns.T.reshape(n_pair, per, n_dev)
+
+    partner = lax.rem(c + 1, n_core)
+    gather_half(partner)
+    u_there[...] = u_wide[...].astype(bf16)
+    to_partner = pltpu.make_async_remote_copy(
+        src_ref=u_there,
+        dst_ref=u_here,
+        send_sem=send_sem.at[6],
+        recv_sem=recv_sem.at[6],
+        device_id={"group": z * n_core + partner, "pair": r},
+        device_id_type=MESH,
+    )
+    to_partner.start()
+    gather_half(c)
+    to_partner.wait_recv()
+    u_out[...] = (u_wide[...] + u_here[...].astype(f32)).astype(bf16)
+    at = z * n_pair + r
+
+    def send_u(plane, pair):
+        pltpu.make_async_remote_copy(
+            src_ref=u_out.at[plane * n_pair + pair],
+            dst_ref=u_in.at[at],
+            send_sem=send_sem.at[5],
+            recv_sem=recv_sem.at[5],
+            device_id={"group": plane * n_core + c, "pair": pair},
+            device_id_type=MESH,
+        ).start()
+
+    for dz in planes:
+        for pair in pairs if dz else pairs[:-1]:
+            send_u(z_at[dz], pair)
+    pltpu.make_async_copy(u_out.at[at], u_in.at[at], recv_sem.at[5]).start()
+    w_t = w_ref[...].T
     tile = 256
     for i in range(rows // tile):
         hg_ref[i * tile : (i + 1) * tile, :] = dot(w_t[i * tile : (i + 1) * tile], pq, 1, 0).astype(bf16)
     all_here(5, u_in)
     total = jnp.sum(u_in[...].astype(f32), axis=0) * inv_root
-    n_b = width // 128
     u_row, u_col = total[:n_b], total[n_b:]
     wide = jnp.concatenate(
         [jnp.where(iota((n_b, 128), 0) == b, u_row, 0.0) for b in range(n_b)], axis=1
@@ -266,7 +337,8 @@
     all_sent(2, key_in, n_pair - 1)
     all_sent(3, score_in, n_dev - 1)
     all_sent(4, value_in, n_dev - 1)
-    all_sent(5, u_in, n_dev - 1)
+    all_sent(5, u_in, half - 1)
+    to_partner.wait_send()
 
 
 def finish_kernel(parts, hg_ref, loss_ref, qg_ref, pg_ref, hg_out, loss_out, qg_out, pg_out, loss_one, sem):
@@ -297,13 +369,14 @@
     slots = n_pair * cap
     k_all = cand * n_pair
     queries_n = n_group * q_rows
+    n_core, side = 2, math.isqrt(n_pair)
     rows = passage_hidden.shape[0]
     per = width // n_dev
     vmem = pl.BlockSpec(memory_space=pltpu.VMEM)
     hbm = pl.BlockSpec(memory_space=pltpu.HBM)
     message = pltpu.VMEM((n_dev, 1, slots), f32)
     results = pl.pallas_call(
-        functools.partial(step_kernel, n_group, n_pair, cap),
+        functools.partial(step_kernel, n_group, n_pair, n_core, side, cap),
         out_shape=(
             pltpu.VMEM((rows, width), bf16),
             pltpu.VMEM((1, 128), f32),
@@ -328,14 +401,21 @@
             message,
             message,
             message,
-            pltpu.VMEM((rows, n_group * slots), bf16),
+            pltpu.VMEM((n_group // n_core, rows, n_core * slots), bf16),
             pltpu.VMEM((k_all, k_all), f32),
-            pltpu.VMEM((n_dev, 16, 128), f32),
-            pltpu.VMEM((n_dev, 16, 128), bf16),
-            pltpu.VMEM((n_dev, 16, 128), bf16),
+            pltpu.VMEM((queries_n, rows), bf16),
+            pltpu.VMEM((queries_n, rows), bf16),
+            pltpu.VMEM((queries_n, rows), bf16),
+            pltpu.VMEM((n_group, q_rows, width), f32),
+            pltpu.VMEM((n_dev // n_core, 16, 128), f32),
+            pltpu.VMEM((n_dev // n_core, 16, 128), bf16),
+            pltpu.VMEM((n_dev // n_core, 16, 128), bf16),
+            pltpu.VMEM((n_dev // n_core, 16, 128), bf16),
+            pltpu.VMEM((n_dev // n_core, 16, 128), bf16),
             pltpu.SemaphoreType.DMA((6,)),
-            pltpu.SemaphoreType.DMA((6,)),
-            pltpu.SemaphoreType.DMA((6,)),
+            pltpu.SemaphoreType.DMA((7,)),
+            pltpu.SemaphoreType.DMA((7,)),
+            pltpu.SemaphoreType.DMA((n_group // n_core,)),
         ],
         compiler_params=pltpu.CompilerParams(
             collective_id=0, has_side_effects=True, vmem_limit_bytes=44 * 2**20

time: 50.2 us -> 46.1 us (0.918)
  Pallas kernels: 49.5 us -> 45.3 us
    pallas_call x1, Pallas kernels: 47.3 us -> 43.2 us  [shards(): pl.pallas_call(functools.partial(step_kernel, n_group, n_pair, n_core, si...]
where the time goes in v4:
time: 46.1 us; the launch traced here: 46 us
  Pallas kernels  45.3 us (98%)
  between operations  0.64 us (1%)
    pallas_call x1, Pallas kernels, shards(): pl.pallas_call(functools.partial(step_kernel, n_group, n_pair, n_core, si...  43.2 us
    pallas_call x1, Pallas kernels, shards(): pl.pallas_call(functools.partial(finish_kernel, parts), out_shape=(jax.Sh...  2.12 us

profile of v4, /device:TPU:1, one launch (start us, length us, event | category | flops | bytes accessed | tf_op | source)
XLA Modules:
  0.0 46.0 jit_solution(9075313593210688303)
XLA Ops:
  0.6 43.2 %step.1 = (bf16[2048,1024]{1,0:T(8,128)(2,1)S(1)}, f32[1,128]{1,0:T(1,128)S(1)}, f32[1,1024]{1,0:T(1,128)S(1)}, f32[8,1024]{1,0:T(8,128)S(1)}) custom-call(bf16[16,1024]{1,0:T(8,128)(2,1)} %bitcast.5, f32[16,32]{1,0:T(8,128)} %bitcast.6, s32[16,32]{1,0:T(8,128)} %bitcast.7, s32[16,32]{1,0:T(8,128)} %bitcast.8, bf16[2048,1024]{1,0:T(8,128)(2,1)} %hid_hbm.1, ...), custom_call_target="tpu_custom_call" | custom-call | tf_op jit(solution)/shard_map/step/pallas_call | solution.py:378
  43.8 2.1 %finish.1 = (bf16[2048,1024]{1,0:T(8,128)(2,1)}, f32[1,1]{1,0:T(1,128)}, f32[1,1024]{1,0:T(1,128)}, f32[8,1024]{1,0:T(8,128)}) custom-call(bf16[2048,1024]{1,0:T(8,128)(2,1)S(1)} %get-tuple-element.12.hg_ref, f32[1,128]{1,0:T(1,128)S(1)} %get-tuple-element.13.loss_ref, f32[1,1024]{1,0:T(1,128)S(1)} %get-tuple-element.14.qg_ref, ...), custom_call_target="tpu_custom_call" | custom-call | tf_op jit(solution)/shard_map/finish/pallas_call | solution.py:438

commit v5 on v4

--- a/solution.py
+++ b/solution.py
@@ -35,8 +35,8 @@
     q_hbm, teach_hbm, owner_hbm, row_hbm, hid_hbm, proj_hbm,
     hg_ref, loss_ref, qg_ref, pg_ref,
     q_ref, teach_ref, owner_ref, row_ref,
-    hid, proj, q_all, req_out, req_in, key_out, key_in, score_out, score_in,
-    value_out, value_in, place, tanh_s, s_hi, s_lo, w_ref, u_ref, u_wide, u_there, u_here, u_out, u_in,
+    hid, proj, pq_own, pq_all, q_all, req_out, req_in, key_out, key_in, score_out, score_in,
+    value_out, value_in, place, tanh_s, s_hi, s_lo, w_ref, u_wide, u_there, u_here, u_out, u_in,
     load_sem, send_sem, recv_sem, plane_sem,
 ):
     n_dev = n_group * n_pair
@@ -153,22 +153,41 @@
         key_out[q, :, cand : 2 * cand] = teach_ref[q : q + 1, :]
 
     loads[3].wait()
+    loads[4].wait()
+    pq_own[...] = (dot(q_ref[...], proj[...], 1, 1) * inv_root).astype(bf16)
+
     pl.semaphore_wait(barrier, n_dev - 1)
 
-    def send_q(i, carry):
-        other = lax.rem(g + i, n_group)
-        pltpu.make_async_remote_copy(
-            src_ref=q_ref,
-            dst_ref=q_all.at[g],
-            send_sem=send_sem.at[0],
-            recv_sem=recv_sem.at[0],
-            device_id={"group": other, "pair": r},
-            device_id_type=MESH,
-        ).start()
-        return carry
-
-    lax.fori_loop(1, n_group, send_q, 0, unroll=True)
-    pltpu.make_async_copy(q_ref, q_all.at[g], recv_sem.at[0]).start()
+    partner = lax.rem(c + 1, n_core)
+    there = {"group": z * n_core + partner, "pair": r}
+
+    few = q_all.at[pl.ds(0, n_plane)]
+
+    def spread_rows(source, target, first, second):
+        def send(what, group, sem, where):
+            pltpu.make_async_remote_copy(
+                src_ref=what,
+                dst_ref=target.at[group],
+                send_sem=send_sem.at[sem],
+                recv_sem=recv_sem.at[sem],
+                device_id=where,
+                device_id_type=MESH,
+            ).start()
+
+        for dz in planes[:-1]:
+            send(source, g, first, {"group": z_at[dz] * n_core + c, "pair": r})
+        send(source, g, second, there)
+        pltpu.make_async_copy(source, target.at[g], recv_sem.at[first]).start()
+
+        def forward():
+            pltpu.make_async_copy(few, few, recv_sem.at[first]).wait()
+            for dz in planes[:-1]:
+                group = z_at[dz] * n_core + c
+                send(target.at[group], group, second, there)
+
+        return forward
+
+    forward_pq = spread_rows(pq_own, pq_all, 0, 7)
     for dz in planes:
         send_plane(dz, send_sem.at[1], recv_sem.at[1], lambda *p: req_out.at[index_of(*p)], req_in, me)
 
@@ -187,12 +206,12 @@
     lax.fori_loop(1, n_pair, send_key, 0, unroll=True)
     pltpu.make_async_copy(key_out.at[r], key_in.at[r], recv_sem.at[2]).start()
 
-    all_here(0, q_all)
-    loads[4].wait()
+    forward_pq()
+
+    pltpu.make_async_copy(few, few, recv_sem.at[7]).wait()
+    loads[5].wait()
     queries_n = n_group * q_rows
-    q_flat = q_all[...].reshape(queries_n, width)
-    pq = (dot(q_flat, proj[...], 1, 1) * inv_root).astype(bf16)
-    loads[5].wait()
+    pq = pq_all[...].reshape(queries_n, width)
     s_t = dot(pq, hid[...], 1, 1)
     s_hi[...], s_lo[...] = halves(s_t)
 
@@ -202,7 +221,9 @@
         asked = req_in[pl.ds(z_at[dz] * in_plane, in_plane)].reshape(n_core, n_pair, 1, slots)
         asked = jnp.sum(asked, axis=1).astype(i32)
         here = jnp.concatenate([asked[i] for i in range(n_core)], axis=1)
-        mark = jnp.where(iota((rows, s_plane), 0) == (here >> 4) - 16, 1.0, 0.0).astype(bf16)
+        wanted = jnp.broadcast_to((here >> 4) - 16, (16, s_plane)).astype(jnp.int16)
+        wanted = jnp.broadcast_to(wanted[None], (rows // 16, 16, s_plane)).reshape(rows, s_plane)
+        mark = jnp.where(iota((rows, s_plane), 0).astype(jnp.int16) == wanted, bf16(1.0), bf16(0.0))
         place[n] = mark
         of_plane = pl.ds(pl.multiple_of(z_at[dz] * q_plane, q_plane), q_plane)
         picks = dot(jnp.concatenate([s_hi[of_plane, :], s_lo[of_plane, :]], axis=0), mark, 1, 0)
@@ -233,6 +254,7 @@
         [jnp.sum(jnp.tanh(t_col - teach[:, a:b]), axis=0, keepdims=True) for a, b in blocks], axis=1
     )
     all_here(3, score_in)
+    forward_q = spread_rows(q_ref, q_all, 8, 9)
     t_hi, t_lo = halves(score_in[:, 0, :].T)
     picked = dot(jnp.concatenate([t_hi, t_lo], axis=0), k_owner, 1, 0)
     s_k = jnp.sum((picked[:slots] + picked[slots:]) * k_slot, axis=0, keepdims=True)
@@ -268,36 +290,32 @@
         spread = jnp.concatenate([jnp.where(row_of == i, back, 0.0) for i in range(n_core)], axis=1)
         of_plane = pl.ds(pl.multiple_of(z_at[dz] * q_plane, q_plane), q_plane)
         w_ref[of_plane, :] = dot(spread.astype(bf16), place[n], 1, 1).astype(bf16)
-    u_ref[...] = dot(w_ref[...], hid[...], 1, 0).reshape(n_group, q_rows, width)
     per = width // n_dev
     n_b = width // 128
-
-    def gather_half(core):
-        for plane in range(n_plane):
-            group = plane * n_core + core
-            of_rows = u_ref[group]
-            for b in range(n_b):
-                u_wide[plane * n_pair : (plane + 1) * n_pair, b, :] = of_rows[:, b * 128 : (b + 1) * 128]
-            width_group = n_pair * per
-            lanes = pl.ds(pl.multiple_of(group * width_group, width_group), width_group)
-            columns = u_ref[:, :, lanes].reshape(n_dev, width_group)
-            u_wide[plane * n_pair : (plane + 1) * n_pair, n_b:, :] = columns.T.reshape(n_pair, per, n_dev)
-
-    partner = lax.rem(c + 1, n_core)
-    gather_half(partner)
-    u_there[...] = u_wide[...].astype(bf16)
+    width_group = n_pair * per
+    width_plane = n_core * width_group
+    for plane in range(n_plane):
+        u = dot(w_ref[...], hid[:, plane * width_plane : (plane + 1) * width_plane], 1, 0)
+        by_group = u.reshape(n_plane, n_core, q_rows, width_plane)
+        for core in range(n_core):
+            columns = u[:, core * width_group : (core + 1) * width_group]
+            u_wide[core, plane * n_pair : (plane + 1) * n_pair, n_b:, :] = columns.T.reshape(n_pair, per, n_dev)
+            for i in range(width_plane // 128):
+                b = plane * (width_plane // 128) + i
+                u_wide[core, :, b, :] = by_group[:, core, :, i * 128 : (i + 1) * 128].reshape(half, 128)
+
+    u_there[...] = u_wide[partner].astype(bf16)
     to_partner = pltpu.make_async_remote_copy(
         src_ref=u_there,
         dst_ref=u_here,
         send_sem=send_sem.at[6],
         recv_sem=recv_sem.at[6],
-        device_id={"group": z * n_core + partner, "pair": r},
+        device_id=there,
         device_id_type=MESH,
     )
     to_partner.start()
-    gather_half(c)
     to_partner.wait_recv()
-    u_out[...] = (u_wide[...] + u_here[...].astype(f32)).astype(bf16)
+    u_out[...] = (u_wide[c] + u_here[...].astype(f32)).astype(bf16)
     at = z * n_pair + r
 
     def send_u(plane, pair):
@@ -314,6 +332,7 @@
         for pair in pairs if dz else pairs[:-1]:
             send_u(z_at[dz], pair)
     pltpu.make_async_copy(u_out.at[at], u_in.at[at], recv_sem.at[5]).start()
+    forward_q()
     w_t = w_ref[...].T
     tile = 256
     for i in range(rows // tile):
@@ -328,11 +347,15 @@
     query_grad = dot(jnp.concatenate([w_hi, w_lo], axis=0), proj[...], 1, 0)
     qg_ref[...] = jnp.sum(query_grad, axis=0, keepdims=True)
     c_hi, c_lo = halves(u_col)
+    pltpu.make_async_copy(few, few, recv_sem.at[9]).wait()
+    q_flat = q_all[...].reshape(queries_n, width)
     proj_grad = dot(jnp.concatenate([c_hi, c_lo], axis=0), q_flat, 1, 0)
     pg_ref[...] = proj_grad[:per] + proj_grad[per:]
 
-    part = q_all.at[pl.ds(0, n_group - 1)]
-    pltpu.make_async_copy(part, part, send_sem.at[0]).wait()
+    all_sent(0, q_all, n_plane - 1)
+    all_sent(7, q_all, n_plane)
+    all_sent(8, q_all, n_plane - 1)
+    all_sent(9, q_all, n_plane)
     all_sent(1, req_in, n_dev - 1)
     all_sent(2, key_in, n_pair - 1)
     all_sent(3, score_in, n_dev - 1)
@@ -392,6 +415,8 @@
             pltpu.VMEM((q_rows, cand), i32),
             pltpu.VMEM((rows, width), bf16),
             pltpu.VMEM((width, width), bf16),
+            pltpu.VMEM((q_rows, width), bf16),
+            pltpu.VMEM((n_group, q_rows, width), bf16),
             pltpu.VMEM((n_group, q_rows, width), bf16),
             message,
             message,
@@ -406,15 +431,14 @@
             pltpu.VMEM((queries_n, rows), bf16),
             pltpu.VMEM((queries_n, rows), bf16),
             pltpu.VMEM((queries_n, rows), bf16),
-            pltpu.VMEM((n_group, q_rows, width), f32),
-            pltpu.VMEM((n_dev // n_core, 16, 128), f32),
+            pltpu.VMEM((n_core, n_dev // n_core, 16, 128), f32),
             pltpu.VMEM((n_dev // n_core, 16, 128), bf16),
             pltpu.VMEM((n_dev // n_core, 16, 128), bf16),
             pltpu.VMEM((n_dev // n_core, 16, 128), bf16),
             pltpu.VMEM((n_dev // n_core, 16, 128), bf16),
             pltpu.SemaphoreType.DMA((6,)),
-            pltpu.SemaphoreType.DMA((7,)),
-            pltpu.SemaphoreType.DMA((7,)),
+            pltpu.SemaphoreType.DMA((10,)),
+            pltpu.SemaphoreType.DMA((10,)),
             pltpu.SemaphoreType.DMA((n_group // n_core,)),
         ],
         compiler_params=pltpu.CompilerParams(

time: 46.1 us -> 44.4 us (0.963)
  Pallas kernels: 45.3 us -> 43.7 us
    pallas_call x1, Pallas kernels: 43.2 us -> 41.5 us  [shards(): pl.pallas_call(functools.partial(step_kernel, n_group, n_pair, n_core, si...]
where the time goes in v5:
time: 44.4 us; the launch traced here: 44.3 us
  Pallas kernels  43.7 us (98%)
  between operations  0.64 us (1%)
    pallas_call x1, Pallas kernels, shards(): pl.pallas_call(functools.partial(step_kernel, n_group, n_pair, n_core, si...  41.5 us
    pallas_call x1, Pallas kernels, shards(): pl.pallas_call(functools.partial(finish_kernel, parts), out_shape=(jax.Sh...  2.12 us

profile of v5, /device:TPU:1, one launch (start us, length us, event | category | flops | bytes accessed | tf_op | source)
XLA Modules:
  0.0 44.3 jit_solution(8108250968398721606)
XLA Ops:
  0.6 41.5 %step.1 = (bf16[2048,1024]{1,0:T(8,128)(2,1)S(1)}, f32[1,128]{1,0:T(1,128)S(1)}, f32[1,1024]{1,0:T(1,128)S(1)}, f32[8,1024]{1,0:T(8,128)S(1)}) custom-call(bf16[16,1024]{1,0:T(8,128)(2,1)} %bitcast.5, f32[16,32]{1,0:T(8,128)} %bitcast.6, s32[16,32]{1,0:T(8,128)} %bitcast.7, s32[16,32]{1,0:T(8,128)} %bitcast.8, bf16[2048,1024]{1,0:T(8,128)(2,1)} %hid_hbm.1, ...), custom_call_target="tpu_custom_call" | custom-call | tf_op jit(solution)/shard_map/step/pallas_call | solution.py:401
  42.2 2.1 %finish.1 = (bf16[2048,1024]{1,0:T(8,128)(2,1)}, f32[1,1]{1,0:T(1,128)}, f32[1,1024]{1,0:T(1,128)}, f32[8,1024]{1,0:T(8,128)}) custom-call(bf16[2048,1024]{1,0:T(8,128)(2,1)S(1)} %get-tuple-element.12.hg_ref, f32[1,128]{1,0:T(1,128)S(1)} %get-tuple-element.13.loss_ref, f32[1,1024]{1,0:T(1,128)S(1)} %get-tuple-element.14.qg_ref, ...), custom_call_target="tpu_custom_call" | custom-call | tf_op jit(solution)/shard_map/finish/pallas_call | solution.py:462

commit v6 on v5

--- a/solution.py
+++ b/solution.py
@@ -33,10 +33,10 @@
 def step_kernel(
     n_group, n_pair, n_core, side, cap,
     q_hbm, teach_hbm, owner_hbm, row_hbm, hid_hbm, proj_hbm,
-    hg_ref, loss_ref, qg_ref, pg_ref,
+    hg_ref, loss_ref, total_ref, proj, q_out,
     q_ref, teach_ref, owner_ref, row_ref,
-    hid, proj, pq_own, pq_all, q_all, req_out, req_in, key_out, key_in, score_out, score_in,
-    value_out, value_in, place, tanh_s, s_hi, s_lo, w_ref, u_wide, u_there, u_here, u_out, u_in,
+    hid, pq_own, pq_all, q_all, req_out, req_in, key_out, key_in, score_out, score_in,
+    value_out, value_in, place, slopes, s_hi, s_lo, w_ref, u_wide, u_there, u_here, u_out, u_in,
     load_sem, send_sem, recv_sem, plane_sem,
 ):
     n_dev = n_group * n_pair
@@ -259,22 +259,19 @@
     picked = dot(jnp.concatenate([t_hi, t_lo], axis=0), k_owner, 1, 0)
     s_k = jnp.sum((picked[:slots] + picked[slots:]) * k_slot, axis=0, keepdims=True)
     s_col = column(s_k)
-    sums = []
+    sums, slope_sums = [], []
     for a, b in blocks:
         soft = jnp.tanh(s_col - s_k[:, a:b])
-        tanh_s[:, a:b] = soft
+        slope = 1.0 - soft * soft
+        slopes[:, a:b] = slope
         sums.append(jnp.sum(soft, axis=0, keepdims=True))
+        slope_sums.append(jnp.sum(slope, axis=0, keepdims=True))
     gap = 0.5 * (jnp.concatenate(sums, axis=1) - t_sum)
     loss_ref[...] = jnp.broadcast_to(6.0 * jnp.sum(gap * gap, axis=1, keepdims=True) / den, (1, 128))
     grad = gap * (loss_scale * 12.0 / den)
     g_col = column(grad)
-    parts = []
-    for a, b in blocks:
-        soft = tanh_s[:, a:b]
-        parts.append(
-            jnp.sum((g_col - grad[:, a:b]) * (1.0 - soft * soft), axis=0, keepdims=True)
-        )
-    s_grad = 0.5 * jnp.concatenate(parts, axis=1)
+    parts = [jnp.sum(g_col * slopes[:, a:b], axis=0, keepdims=True) for a, b in blocks]
+    s_grad = 0.5 * (jnp.concatenate(parts, axis=1) - grad * jnp.concatenate(slope_sums, axis=1))
     value_out[:, 0, :] = dot(k_owner, (k_slot * s_grad).astype(bf16), 1, 1)
     for dz in planes:
         send_plane(
@@ -337,20 +334,10 @@
     tile = 256
     for i in range(rows // tile):
         hg_ref[i * tile : (i + 1) * tile, :] = dot(w_t[i * tile : (i + 1) * tile], pq, 1, 0).astype(bf16)
+    pltpu.make_async_copy(few, few, recv_sem.at[9]).wait()
+    q_out[...] = q_all[...].reshape(queries_n, width)
     all_here(5, u_in)
-    total = jnp.sum(u_in[...].astype(f32), axis=0) * inv_root
-    u_row, u_col = total[:n_b], total[n_b:]
-    wide = jnp.concatenate(
-        [jnp.where(iota((n_b, 128), 0) == b, u_row, 0.0) for b in range(n_b)], axis=1
-    )
-    w_hi, w_lo = halves(wide)
-    query_grad = dot(jnp.concatenate([w_hi, w_lo], axis=0), proj[...], 1, 0)
-    qg_ref[...] = jnp.sum(query_grad, axis=0, keepdims=True)
-    c_hi, c_lo = halves(u_col)
-    pltpu.make_async_copy(few, few, recv_sem.at[9]).wait()
-    q_flat = q_all[...].reshape(queries_n, width)
-    proj_grad = dot(jnp.concatenate([c_hi, c_lo], axis=0), q_flat, 1, 0)
-    pg_ref[...] = proj_grad[:per] + proj_grad[per:]
+    total_ref[...] = jnp.sum(u_in[...].astype(f32), axis=0) * inv_root
 
     all_sent(0, q_all, n_plane - 1)
     all_sent(7, q_all, n_plane)
@@ -364,13 +351,12 @@
     to_partner.wait_send()
 
 
-def finish_kernel(parts, hg_ref, loss_ref, qg_ref, pg_ref, hg_out, loss_out, qg_out, pg_out, loss_one, sem):
-    loss_one[...] = loss_ref[:, 0:1]
+def finish_kernel(
+    parts, hg_ref, loss_ref, total_ref, proj, queries, hg_out, loss_out, qg_out, pg_out,
+    loss_one, qg_ref, pg_ref, sem,
+):
     tile = hg_ref.shape[0] // parts
     stores = [
-        pltpu.make_async_copy(source, target, sem.at[parts + n])
-        for n, (source, target) in enumerate([(loss_one, loss_out), (qg_ref, qg_out), (pg_ref, pg_out)])
-    ] + [
         pltpu.make_async_copy(
             hg_ref.at[pl.ds(i * tile, tile)], hg_out.at[pl.ds(i * tile, tile)], sem.at[i]
         )
@@ -378,6 +364,23 @@
     ]
     for store in stores:
         store.start()
+    loss_one[...] = loss_ref[:, 0:1]
+    n_b = proj.shape[0] // 128
+    u_row, u_col = total_ref[:n_b], total_ref[n_b:]
+    wide = jnp.concatenate(
+        [jnp.where(iota((n_b, 128), 0) == b, u_row, 0.0) for b in range(n_b)], axis=1
+    )
+    w_hi, w_lo = halves(wide)
+    query_grad = dot(jnp.concatenate([w_hi, w_lo], axis=0), proj[...], 1, 0)
+    qg_ref[...] = jnp.sum(query_grad, axis=0, keepdims=True)
+    c_hi, c_lo = halves(u_col)
+    proj_grad = dot(jnp.concatenate([c_hi, c_lo], axis=0), queries[...], 1, 0)
+    per = pg_ref.shape[0]
+    pg_ref[...] = proj_grad[:per] + proj_grad[per:]
+    for n, (source, target) in enumerate([(loss_one, loss_out), (qg_ref, qg_out), (pg_ref, pg_out)]):
+        store = pltpu.make_async_copy(source, target, sem.at[parts + n])
+        store.start()
+        stores.append(store)
     for store in stores:
         store.wait()
 
@@ -403,18 +406,18 @@
         out_shape=(
             pltpu.VMEM((rows, width), bf16),
             pltpu.VMEM((1, 128), f32),
-            pltpu.VMEM((1, width), f32),
-            pltpu.VMEM((per, width), f32),
+            pltpu.VMEM((16, 128), f32),
+            pltpu.VMEM((width, width), bf16),
+            pltpu.VMEM((queries_n, width), bf16),
         ),
         in_specs=[hbm] * 6,
-        out_specs=(vmem,) * 4,
+        out_specs=(vmem,) * 5,
         scratch_shapes=[
             pltpu.VMEM((q_rows, width), bf16),
             pltpu.VMEM((q_rows, cand), f32),
             pltpu.VMEM((q_rows, cand), i32),
             pltpu.VMEM((q_rows, cand), i32),
             pltpu.VMEM((rows, width), bf16),
-            pltpu.VMEM((width, width), bf16),
             pltpu.VMEM((q_rows, width), bf16),
             pltpu.VMEM((n_group, q_rows, width), bf16),
             pltpu.VMEM((n_group, q_rows, width), bf16),
@@ -467,9 +470,14 @@
             jax.ShapeDtypeStruct((1, width), f32),
             jax.ShapeDtypeStruct((per, width), f32),
         ),
-        in_specs=[vmem] * 4,
+        in_specs=[vmem] * 5,
         out_specs=(hbm,) * 4,
-        scratch_shapes=[pltpu.VMEM((1, 1), f32), pltpu.SemaphoreType.DMA((parts + 3,))],
+        scratch_shapes=[
+            pltpu.VMEM((1, 1), f32),
+            pltpu.VMEM((1, width), f32),
+            pltpu.VMEM((per, width), f32),
+            pltpu.SemaphoreType.DMA((parts + 3,)),
+        ],
         compiler_params=pltpu.CompilerParams(vmem_limit_bytes=4 * 2**20),
         name="finish",
     )(*results)

time: 44.4 us -> 43.9 us (0.989)
  Pallas kernels: 43.7 us -> 43.1 us
    pallas_call x1, Pallas kernels: 41.5 us -> 41 us  [shards(): pl.pallas_call(functools.partial(step_kernel, n_group, n_pair, n_core, si...]
where the time goes in v6:
time: 43.9 us; the launch traced here: 43.8 us
  Pallas kernels  43.1 us (98%)
  between operations  0.64 us (1%)
    pallas_call x1, Pallas kernels, shards(): pl.pallas_call(functools.partial(step_kernel, n_group, n_pair, n_core, si...  41 us
    pallas_call x1, Pallas kernels, shards(): pl.pallas_call(functools.partial(finish_kernel, parts), out_shape=(jax.Sh...  2.11 us

profile of v6, /device:TPU:1, one launch (start us, length us, event | category | flops | bytes accessed | tf_op | source)
XLA Modules:
  0.0 43.8 jit_solution(7788875786575289147)
XLA Ops:
  0.6 41.0 %step.1 = (bf16[2048,1024]{1,0:T(8,128)(2,1)S(1)}, f32[1,128]{1,0:T(1,128)S(1)}, f32[16,128]{1,0:T(8,128)S(1)}, bf16[1024,1024]{1,0:T(8,128)(2,1)S(1)}, bf16[128,1024]{1,0:T(8,128)(2,1)S(1)}) custom-call(bf16[16,1024]{1,0:T(8,128)(2,1)} %bitcast.5, f32[16,32]{1,0:T(8,128)} %bitcast.6, s32[16,32]{1,0:T(8,128)} %bitcast.7, s32[16,32]{1,0:T(8,128)} %bitcast.8, ...), custom_call_target="tpu_custom_call" | custom-call | tf_op jit(solution)/shard_map/step/pallas_call | solution.py:404
  41.6 2.1 %finish.1 = (bf16[2048,1024]{1,0:T(8,128)(2,1)}, f32[1,1]{1,0:T(1,128)}, f32[1,1024]{1,0:T(1,128)}, f32[8,1024]{1,0:T(8,128)}) custom-call(bf16[2048,1024]{1,0:T(8,128)(2,1)S(1)} %get-tuple-element.13.hg_ref, f32[1,128]{1,0:T(1,128)S(1)} %get-tuple-element.14.loss_ref, f32[16,128]{1,0:T(8,128)S(1)} %get-tuple-element.15.total_ref, ...), custom_call_target="tpu_custom_call" | custom-call | tf_op jit(solution)/shard_map/finish/pallas_call | solution.py:465

commit v7 on v6

--- a/solution.py
+++ b/solution.py
@@ -37,7 +37,7 @@
     q_ref, teach_ref, owner_ref, row_ref,
     hid, pq_own, pq_all, q_all, req_out, req_in, key_out, key_in, score_out, score_in,
     value_out, value_in, place, slopes, s_hi, s_lo, w_ref, u_wide, u_there, u_here, u_out, u_in,
-    load_sem, send_sem, recv_sem, plane_sem,
+    load_sem, send_sem, recv_sem, plane_sem, pair_send, pair_recv,
 ):
     n_dev = n_group * n_pair
     q_rows, width = q_ref.shape
@@ -301,18 +301,19 @@
                 b = plane * (width_plane // 128) + i
                 u_wide[core, :, b, :] = by_group[:, core, :, i * 128 : (i + 1) * 128].reshape(half, 128)
 
-    u_there[...] = u_wide[partner].astype(bf16)
-    to_partner = pltpu.make_async_remote_copy(
-        src_ref=u_there,
-        dst_ref=u_here,
-        send_sem=send_sem.at[6],
-        recv_sem=recv_sem.at[6],
-        device_id=there,
-        device_id_type=MESH,
-    )
-    to_partner.start()
-    to_partner.wait_recv()
-    u_out[...] = (u_wide[c] + u_here[...].astype(f32)).astype(bf16)
+    passed = {}
+    for dz in planes:
+        of_plane = pl.ds(z_at[dz] * n_pair, n_pair)
+        u_there[of_plane] = u_wide[partner, of_plane].astype(bf16)
+        passed[dz] = pltpu.make_async_remote_copy(
+            src_ref=u_there.at[of_plane],
+            dst_ref=u_here.at[of_plane],
+            send_sem=pair_send.at[dz],
+            recv_sem=pair_recv.at[dz],
+            device_id=there,
+            device_id_type=MESH,
+        )
+        passed[dz].start()
     at = z * n_pair + r
 
     def send_u(plane, pair):
@@ -326,6 +327,9 @@
         ).start()
 
     for dz in planes:
+        of_plane = pl.ds(z_at[dz] * n_pair, n_pair)
+        passed[dz].wait_recv()
+        u_out[of_plane] = (u_wide[c, of_plane] + u_here[of_plane].astype(f32)).astype(bf16)
         for pair in pairs if dz else pairs[:-1]:
             send_u(z_at[dz], pair)
     pltpu.make_async_copy(u_out.at[at], u_in.at[at], recv_sem.at[5]).start()
@@ -348,7 +352,8 @@
     all_sent(3, score_in, n_dev - 1)
     all_sent(4, value_in, n_dev - 1)
     all_sent(5, u_in, half - 1)
-    to_partner.wait_send()
+    for copy in passed.values():
+        copy.wait_send()
 
 
 def finish_kernel(
@@ -443,6 +448,8 @@
             pltpu.SemaphoreType.DMA((10,)),
             pltpu.SemaphoreType.DMA((10,)),
             pltpu.SemaphoreType.DMA((n_group // n_core,)),
+            pltpu.SemaphoreType.DMA((n_group // n_core,)),
+            pltpu.SemaphoreType.DMA((n_group // n_core,)),
         ],
         compiler_params=pltpu.CompilerParams(
             collective_id=0, has_side_effects=True, vmem_limit_bytes=44 * 2**20

time: 43.9 us -> 43.5 us (level)
  no operation moved by 1% of the time
where the time goes in v7:
time: 43.5 us; the launch traced here: 43.4 us
  Pallas kernels  42.8 us (98%)
  between operations  0.64 us (1%)
    pallas_call x1, Pallas kernels, shards(): pl.pallas_call(functools.partial(step_kernel, n_group, n_pair, n_core, si...  40.7 us
    pallas_call x1, Pallas kernels, shards(): pl.pallas_call(functools.partial(finish_kernel, parts), out_shape=(jax.Sh...  2.11 us

profile of v7, /device:TPU:1, one launch (start us, length us, event | category | flops | bytes accessed | tf_op | source)
XLA Modules:
  0.0 43.4 jit_solution(11683374560187929170)
XLA Ops:
  0.6 40.7 %step.1 = (bf16[2048,1024]{1,0:T(8,128)(2,1)S(1)}, f32[1,128]{1,0:T(1,128)S(1)}, f32[16,128]{1,0:T(8,128)S(1)}, bf16[1024,1024]{1,0:T(8,128)(2,1)S(1)}, bf16[128,1024]{1,0:T(8,128)(2,1)S(1)}) custom-call(bf16[16,1024]{1,0:T(8,128)(2,1)} %bitcast.5, f32[16,32]{1,0:T(8,128)} %bitcast.6, s32[16,32]{1,0:T(8,128)} %bitcast.7, s32[16,32]{1,0:T(8,128)} %bitcast.8, ...), custom_call_target="tpu_custom_call" | custom-call | tf_op jit(solution)/shard_map/step/pallas_call | solution.py:409
  41.3 2.1 %finish.1 = (bf16[2048,1024]{1,0:T(8,128)(2,1)}, f32[1,1]{1,0:T(1,128)}, f32[1,1024]{1,0:T(1,128)}, f32[8,1024]{1,0:T(8,128)}) custom-call(bf16[2048,1024]{1,0:T(8,128)(2,1)S(1)} %get-tuple-element.13.hg_ref, f32[1,128]{1,0:T(1,128)S(1)} %get-tuple-element.14.loss_ref, f32[16,128]{1,0:T(8,128)S(1)} %get-tuple-element.15.total_ref, ...), custom_call_target="tpu_custom_call" | custom-call | tf_op jit(solution)/shard_map/finish/pallas_call | solution.py:472

commit v8 on v7

--- a/solution.py
+++ b/solution.py
@@ -63,8 +63,6 @@
              (proj_hbm, proj), (hid_hbm, hid)]
         )
     ]
-    for load in loads:
-        load.start()
 
     z, c = g // n_core, lax.rem(g, n_core)
     y, x = r // side, lax.rem(r, side)
@@ -102,7 +100,10 @@
             barrier, inc=1, device_id={"group": group, "pair": pair}, device_id_type=MESH
         )
 
-    for dz in planes:
+    plane_peers(planes[0], greet)
+    for load in loads:
+        load.start()
+    for dz in planes[1:]:
         plane_peers(dz, greet)
 
     def send_plane(dz, send, recv, source_of, target, at):
@@ -468,7 +469,7 @@
             )
         )
     )
-    parts = 8
+    parts = 4
     hidden_grad, loss, query_grad, projection_grad = pl.pallas_call(
         functools.partial(finish_kernel, parts),
         out_shape=(

time: 43.5 us -> 43.5 us (level)
  no operation moved by 1% of the time
where the time goes in v8:
time: 43.5 us; the launch traced here: 43.4 us
  Pallas kernels  42.8 us (98%)
  between operations  0.64 us (1%)
    pallas_call x1, Pallas kernels, shards(): pl.pallas_call(functools.partial(step_kernel, n_group, n_pair, n_core, si...  40.7 us
    pallas_call x1, Pallas kernels, shards(): pl.pallas_call(functools.partial(finish_kernel, parts), out_shape=(jax.Sh...  2.08 us

profile of v8, /device:TPU:1, one launch (start us, length us, event | category | flops | bytes accessed | tf_op | source)
XLA Modules:
  0.0 43.4 jit_solution(2623584837145611567)
XLA Ops:
  0.6 40.7 %step.1 = (bf16[2048,1024]{1,0:T(8,128)(2,1)S(1)}, f32[1,128]{1,0:T(1,128)S(1)}, f32[16,128]{1,0:T(8,128)S(1)}, bf16[1024,1024]{1,0:T(8,128)(2,1)S(1)}, bf16[128,1024]{1,0:T(8,128)(2,1)S(1)}) custom-call(bf16[16,1024]{1,0:T(8,128)(2,1)} %bitcast.5, f32[16,32]{1,0:T(8,128)} %bitcast.6, s32[16,32]{1,0:T(8,128)} %bitcast.7, s32[16,32]{1,0:T(8,128)} %bitcast.8, ...), custom_call_target="tpu_custom_call" | custom-call | tf_op jit(solution)/shard_map/step/pallas_call | solution.py:410
  41.3 2.1 %finish.1 = (bf16[2048,1024]{1,0:T(8,128)(2,1)}, f32[1,1]{1,0:T(1,128)}, f32[1,1024]{1,0:T(1,128)}, f32[8,1024]{1,0:T(8,128)}) custom-call(bf16[2048,1024]{1,0:T(8,128)(2,1)S(1)} %get-tuple-element.13.hg_ref, f32[1,128]{1,0:T(1,128)S(1)} %get-tuple-element.14.loss_ref, f32[16,128]{1,0:T(8,128)S(1)} %get-tuple-element.15.total_ref, ...), custom_call_target="tpu_custom_call" | custom-call | tf_op jit(solution)/shard_map/finish/pallas_call | solution.py:473
